TPU v7x, 512 devices: a whole 4x4x16 slice. The times are simulated.
512 devices in a mesh: bl: 32 (over y, x, core), dir: 16 (over z).
Axes of the slice: x: 4, y: 4, z: 16, core: 2. Of those that a mesh axis runs over, the one named last changes fastest.
Arguments:
- visibilities: float32 [8, 16, 8192], P(None, 'dir', 'bl'), may hold values from -24 to 24
- coherencies: bfloat16 [32, 8, 16, 8192], P('dir', None, None, 'bl'), may hold values from -6 to 6
- gain_offsets: float32 [32, 8, 512], P(None, None, 'bl'), may hold values from -1.5 to 1.5
- stations: int32 [2, 8192], P(None, 'bl'), may hold values from 0 to 511, as said below
- solve_order: int32 [32], replicated, may hold values from 0 to 31, each once
- counts: int32 [32], replicated, may hold values from 1 to 2
- damping: int32 [32], replicated, may hold values from 1 to 8
Outputs:
- gains: float32 [32, 8, 512], P(None, None, 'bl')
- residual: float32 [8, 16, 8192], P(None, 'dir', 'bl')
Inputs may be any that keep to these rules, and one draw needn't show every extreme that they name: Each baseline names two different stations. `solve_order`: each direction appears once.
All inputs are finite; a program needn't handle non-finite values.
Results may differ from a plain program's by a relative error of at most 0.0003.
Values may be sent and summed in bfloat16 or wider, within the bound.
A program may use at most 64 MiB of HBM per device.

v0:
```python
import jax
import jax.numpy as jnp
from jax import lax
from jax.sharding import PartitionSpec as P

LM_ITERS = 2
SOLVED = 4


def from_root(shard, axis, root):
    mine = lax.axis_index(axis) == root
    return lax.psum(jnp.where(mine, shard, jnp.zeros_like(shard)), axis)


def matrix_entry(mat, i, j):
    return (mat[4 * i + 2 * j], mat[4 * i + 2 * j + 1])


def matmul_two(left, right):
    pieces = []
    for i in (0, 1):
        for j in (0, 1):
            left_r0, left_i0 = matrix_entry(left, i, 0)
            left_r1, left_i1 = matrix_entry(left, i, 1)
            right_r0, right_i0 = matrix_entry(right, 0, j)
            right_r1, right_i1 = matrix_entry(right, 1, j)
            pieces.append(
                left_r0 * right_r0 - left_i0 * right_i0 + left_r1 * right_r1 - left_i1 * right_i1
            )
            pieces.append(
                left_r0 * right_i0 + left_i0 * right_r0 + left_r1 * right_i1 + left_i1 * right_r1
            )
    return jnp.stack(pieces)


def adjoint(mat):
    return jnp.stack([mat[0], -mat[1], mat[4], -mat[5], mat[2], -mat[3], mat[6], -mat[7]])


def apply_gains(gain_p, coher_now, gain_q):
    return matmul_two(matmul_two(gain_p, coher_now), adjoint(gain_q))


def gram_parts(gram):
    return jnp.stack([gram[0], gram[6], gram[2], gram[3]])


def station_terms(gain_p, gain_q, coher_now, target):
    z_rows = matmul_two(coher_now, adjoint(gain_q))
    y_rows = matmul_two(adjoint(coher_now), adjoint(gain_p))
    leading_endpoint = jnp.concatenate(
        [matmul_two(target, adjoint(z_rows)), gram_parts(matmul_two(z_rows, adjoint(z_rows)))], 0
    )
    second = jnp.concatenate(
        [
            matmul_two(adjoint(target), adjoint(y_rows)),
            gram_parts(matmul_two(y_rows, adjoint(y_rows))),
        ],
        0,
    )
    return (jnp.sum(leading_endpoint, axis=1), jnp.sum(second, axis=1))


def solve_station(gathered_sums, gain_now, damp_value):
    numerator = gathered_sums[:8] + damp_value * gain_now
    diag_a = gathered_sums[8] + damp_value
    diag_d = gathered_sums[9] + damp_value
    cross_r = gathered_sums[10]
    cross_i = gathered_sums[11]
    determinant = diag_a * diag_d - cross_r * cross_r - cross_i * cross_i
    zeros_row = jnp.zeros_like(determinant)
    inverse = (
        jnp.stack([diag_d, zeros_row, -cross_r, -cross_i, -cross_r, cross_i, diag_a, zeros_row])
        / determinant
    )
    return matmul_two(numerator, inverse)


def on_device(visibilities, coherencies, gain_offsets, stations, solve_order, counts, damping):
    identity = jnp.zeros((8,), jnp.float32).at[0].set(1.0).at[6].set(1.0)
    start = lax.all_gather(gain_offsets, "bl", axis=2, tiled=True) + identity[None, :, None]
    groups = lax.axis_size("bl")
    channels = visibilities.shape[1]
    total_channels = coherencies.shape[2]
    owned_count = coherencies.shape[0]
    station_count = start.shape[2]
    damping_factor = visibilities.shape[2] * groups * total_channels / station_count
    lane_index = lax.axis_index("dir")
    ends_p = jnp.take(start, stations[0], axis=2)
    ends_q = jnp.take(start, stations[1], axis=2)
    owned_p = lax.dynamic_slice_in_dim(ends_p, lane_index * owned_count, owned_count, 0)
    owned_q = lax.dynamic_slice_in_dim(ends_q, lane_index * owned_count, owned_count, 0)
    gain_p = jnp.transpose(owned_p, (1, 0, 2))[:, :, None, :]
    gain_q = jnp.transpose(owned_q, (1, 0, 2))[:, :, None, :]
    coher_owned = jnp.transpose(coherencies, (1, 0, 2, 3)).astype(jnp.float32)
    partial_value = jnp.sum(apply_gains(gain_p, coher_owned, gain_q), axis=1)
    first_model = lax.psum_scatter(partial_value, "dir", scatter_dimension=1, tiled=True)
    first_residual = visibilities - first_model

    def direction_model(gain_now, coher_now):
        gain_p = jnp.take(gain_now, stations[0], axis=1)[:, None, :]
        gain_q = jnp.take(gain_now, stations[1], axis=1)[:, None, :]
        return apply_gains(gain_p, coher_now, gain_q)

    def sweep(step_index, state):
        gain_table, residual = state
        which = solve_order[step_index]
        owner_row = lax.dynamic_index_in_dim(coherencies, which % owned_count, 0, keepdims=False)
        broadcast_rows = from_root(owner_row, "dir", which // owned_count)
        coher_now = lax.dynamic_slice_in_dim(
            broadcast_rows, lane_index * channels, channels, 1
        ).astype(jnp.float32)
        damp_value = damping[which].astype(jnp.float32) * damping_factor
        gain_start = gain_table[which]
        target = residual + direction_model(gain_start, coher_now)

        def iterate(round_index, gain_now):
            gain_p = jnp.take(gain_now, stations[0], axis=1)[:, None, :]
            gain_q = jnp.take(gain_now, stations[1], axis=1)[:, None, :]
            leading_endpoint, second = station_terms(gain_p, gain_q, coher_now, target)
            local_sums = (
                jax.ops.segment_sum(leading_endpoint.T, stations[0], station_count)
                + jax.ops.segment_sum(second.T, stations[1], station_count)
            ).T
            gathered_sums = lax.psum(local_sums, ("bl", "dir"))
            updated = solve_station(gathered_sums, gain_now, damp_value)
            return jnp.where(round_index < counts[which], updated, gain_now)

        gain_final = lax.fori_loop(0, LM_ITERS, iterate, gain_start)
        residual = target - direction_model(gain_final, coher_now)
        return (gain_table.at[which].set(gain_final), residual)

    gain_table, residual = lax.fori_loop(0, SOLVED, sweep, (start, first_residual))
    own_width = station_count // groups
    gains = lax.dynamic_slice_in_dim(gain_table, lax.axis_index("bl") * own_width, own_width, 2)
    return (gains, residual)


def solution(mesh):
    return jax.shard_map(
        on_device,
        mesh=mesh,
        in_specs=(
            P(None, "dir", "bl"),
            P("dir", None, None, "bl"),
            P(None, None, "bl"),
            P(None, "bl"),
            P(),
            P(),
            P(),
        ),
        out_specs=(P(None, None, "bl"), P(None, "dir", "bl")),
        check_vma=False,
    )
```

profile of v0, /device:TPU:1, one launch (start us, length us, event | category | flops | bytes accessed | tf_op | source)
XLA Modules:
  0.0 1577.5 jit_solution(7976615437648332978)
XLA Ops:
  9.8 29.8 %all_gather.3 = f32[32,8,512]{0,1,2:T(8,128)S(1)} all-gather(f32[32,8,16]{0,1,2:T(8,128)S(1)} %copy.1403), channel_id=1, replica_groups=mesh['bl'=32,'dir'=16] {'bl'}, dimensions={2}, use_global_device_ids=true | all-gather | bytes 540672 | tf_op jit(solution)/shard_map/all_gather | solution.py:81
  48.5 7.5 copy.1415
  56.0 49.5 %reduce-scatter.2.cloned.1.call-done = f32[8,1,256]{2,0,1:T(8,128)} async-done(((f32[8,16,256]{2,0,1:T(8,128)}), f32[8,1,256]{2,0,1:T(8,128)}) %reduce-scatter.2.cloned.1.call-update) | async-done | bytes 8208 | tf_op jit(solution)/shard_map/reduce_scatter | solution.py:97
  106.3 1457.3 %while.54 = (s32[]{:T(128)}, f32[32,8,512]{1,2,0:T(8,128)}, f32[8,1,256]{2,1,0:T(1,128)S(1)}, s32[32]{0:T(128)S(1)}, bf16[2,8,16,256]{3,2,1,0:T(8,128)(2,1)S(1)}...) while((s32[]{:T(128)}, f32[32,8,512]{1,2,0:T(8,128)}, ...), condition=%wide.region_10.13_spmd, body=%wide.region_2.12_spmd.sunk | while | flops 323119 | bytes 2925989 | solution.py:133
  116.9 125.3 %all-reduce.2.cloned.1.call-done = bf16[8,16,256]{2,1,0:T(8,128)(2,1)} async-done(((bf16[8,16,256]{2,1,0:T(8,128)(2,1)}), bf16[8,16,256]{2,1,0:T(8,128)(2,1)}) %all-reduce.2.cloned.1.call-update) | async-done | bytes 65552 | tf_op jit(solution)/shard_map/while/body/eval_jaxpr/psum | solution.py:12
  243.2 235.5 %while.55 = (s32[]{:T(128)}, f32[8,512]{0,1:T(8,128)S(1)}, s32[1]{0:T(128)}, s32[2,256]{1,0:T(2,128)S(1)}, f32[8,1,256]{2,1,0:T(1,128)S(1)}, /*index=5*/f32[8,1,...) while((s32[]{:T(128)}, f32[8,512]{0,1:T(8,128)S(1)}, ...), condition=%wide.region_9.11_spmd, body=%wide.region_5.10_spmd.sunk | while | flops 164865 | bytes 1329347 | solution.py:129
  249.5 112.0 %psum.29 = f32[12,512]{0,1:T(8,128)S(1)} all-reduce(f32[12,512]{0,1:T(8,128)S(1)} %add_bitcast_fusion.2), channel_id=1, replica_groups=mesh['bl'=32,'dir'=16] {'bl','dir'}, use_global_device_ids=true, to_apply=%region_8.9 | all-reduce | flops 6144 | bytes 49152 | tf_op jit(solution)/shard_map/while/body/eval_jaxpr/while/body/eval_jaxpr/psum | solution.py:125
  372.5 101.4 %psum.29 = f32[12,512]{0,1:T(8,128)S(1)} all-reduce(f32[12,512]{0,1:T(8,128)S(1)} %add_bitcast_fusion.2), channel_id=1, replica_groups=mesh['bl'=32,'dir'=16] {'bl','dir'}, use_global_device_ids=true, to_apply=%region_8.9 | all-reduce | flops 6144 | bytes 49152 | tf_op jit(solution)/shard_map/while/body/eval_jaxpr/while/body/eval_jaxpr/psum | solution.py:125
  480.5 2.3 fusion.153
  493.4 109.1 %all-reduce.2.cloned.1.call-done = bf16[8,16,256]{2,1,0:T(8,128)(2,1)} async-done(((bf16[8,16,256]{2,1,0:T(8,128)(2,1)}), bf16[8,16,256]{2,1,0:T(8,128)(2,1)}) %all-reduce.2.cloned.1.call-update) | async-done | bytes 65552 | tf_op jit(solution)/shard_map/while/body/eval_jaxpr/psum | solution.py:12
  603.5 235.5 %while.55 = (s32[]{:T(128)}, f32[8,512]{0,1:T(8,128)S(1)}, s32[1]{0:T(128)}, s32[2,256]{1,0:T(2,128)S(1)}, f32[8,1,256]{2,1,0:T(1,128)S(1)}, /*index=5*/f32[8,1,...) while((s32[]{:T(128)}, f32[8,512]{0,1:T(8,128)S(1)}, ...), condition=%wide.region_9.11_spmd, body=%wide.region_5.10_spmd.sunk | while | flops 164865 | bytes 1329347 | solution.py:129
  609.7 112.0 %psum.29 = f32[12,512]{0,1:T(8,128)S(1)} all-reduce(f32[12,512]{0,1:T(8,128)S(1)} %add_bitcast_fusion.2), channel_id=1, replica_groups=mesh['bl'=32,'dir'=16] {'bl','dir'}, use_global_device_ids=true, to_apply=%region_8.9 | all-reduce | flops 6144 | bytes 49152 | tf_op jit(solution)/shard_map/while/body/eval_jaxpr/while/body/eval_jaxpr/psum | solution.py:125
  732.8 101.4 %psum.29 = f32[12,512]{0,1:T(8,128)S(1)} all-reduce(f32[12,512]{0,1:T(8,128)S(1)} %add_bitcast_fusion.2), channel_id=1, replica_groups=mesh['bl'=32,'dir'=16] {'bl','dir'}, use_global_device_ids=true, to_apply=%region_8.9 | all-reduce | flops 6144 | bytes 49152 | tf_op jit(solution)/shard_map/while/body/eval_jaxpr/while/body/eval_jaxpr/psum | solution.py:125
  853.6 109.1 %all-reduce.2.cloned.1.call-done = bf16[8,16,256]{2,1,0:T(8,128)(2,1)} async-done(((bf16[8,16,256]{2,1,0:T(8,128)(2,1)}), bf16[8,16,256]{2,1,0:T(8,128)(2,1)}) %all-reduce.2.cloned.1.call-update) | async-done | bytes 65552 | tf_op jit(solution)/shard_map/while/body/eval_jaxpr/psum | solution.py:12
  963.7 235.5 %while.55 = (s32[]{:T(128)}, f32[8,512]{0,1:T(8,128)S(1)}, s32[1]{0:T(128)}, s32[2,256]{1,0:T(2,128)S(1)}, f32[8,1,256]{2,1,0:T(1,128)S(1)}, /*index=5*/f32[8,1,...) while((s32[]{:T(128)}, f32[8,512]{0,1:T(8,128)S(1)}, ...), condition=%wide.region_9.11_spmd, body=%wide.region_5.10_spmd.sunk | while | flops 164865 | bytes 1329347 | solution.py:129
  970.0 112.0 %psum.29 = f32[12,512]{0,1:T(8,128)S(1)} all-reduce(f32[12,512]{0,1:T(8,128)S(1)} %add_bitcast_fusion.2), channel_id=1, replica_groups=mesh['bl'=32,'dir'=16] {'bl','dir'}, use_global_device_ids=true, to_apply=%region_8.9 | all-reduce | flops 6144 | bytes 49152 | tf_op jit(solution)/shard_map/while/body/eval_jaxpr/while/body/eval_jaxpr/psum | solution.py:125
  1093.0 101.4 %psum.29 = f32[12,512]{0,1:T(8,128)S(1)} all-reduce(f32[12,512]{0,1:T(8,128)S(1)} %add_bitcast_fusion.2), channel_id=1, replica_groups=mesh['bl'=32,'dir'=16] {'bl','dir'}, use_global_device_ids=true, to_apply=%region_8.9 | all-reduce | flops 6144 | bytes 49152 | tf_op jit(solution)/shard_map/while/body/eval_jaxpr/while/body/eval_jaxpr/psum | solution.py:125
  1201.0 2.3 fusion.153
  1213.9 109.1 %all-reduce.2.cloned.1.call-done = bf16[8,16,256]{2,1,0:T(8,128)(2,1)} async-done(((bf16[8,16,256]{2,1,0:T(8,128)(2,1)}), bf16[8,16,256]{2,1,0:T(8,128)(2,1)}) %all-reduce.2.cloned.1.call-update) | async-done | bytes 65552 | tf_op jit(solution)/shard_map/while/body/eval_jaxpr/psum | solution.py:12
  1324.0 235.5 %while.55 = (s32[]{:T(128)}, f32[8,512]{0,1:T(8,128)S(1)}, s32[1]{0:T(128)}, s32[2,256]{1,0:T(2,128)S(1)}, f32[8,1,256]{2,1,0:T(1,128)S(1)}, /*index=5*/f32[8,1,...) while((s32[]{:T(128)}, f32[8,512]{0,1:T(8,128)S(1)}, ...), condition=%wide.region_9.11_spmd, body=%wide.region_5.10_spmd.sunk | while | flops 164865 | bytes 1329347 | solution.py:129
  1330.2 112.0 %psum.29 = f32[12,512]{0,1:T(8,128)S(1)} all-reduce(f32[12,512]{0,1:T(8,128)S(1)} %add_bitcast_fusion.2), channel_id=1, replica_groups=mesh['bl'=32,'dir'=16] {'bl','dir'}, use_global_device_ids=true, to_apply=%region_8.9 | all-reduce | flops 6144 | bytes 49152 | tf_op jit(solution)/shard_map/while/body/eval_jaxpr/while/body/eval_jaxpr/psum | solution.py:125
  1453.3 101.4 %psum.29 = f32[12,512]{0,1:T(8,128)S(1)} all-reduce(f32[12,512]{0,1:T(8,128)S(1)} %add_bitcast_fusion.2), channel_id=1, replica_groups=mesh['bl'=32,'dir'=16] {'bl','dir'}, use_global_device_ids=true, to_apply=%region_8.9 | all-reduce | flops 6144 | bytes 49152 | tf_op jit(solution)/shard_map/while/body/eval_jaxpr/while/body/eval_jaxpr/psum | solution.py:125
  1561.3 2.3 fusion.153
  1563.6 6.7 copy.1417
  (794 shorter events, 130.7 us)
Async XLA Ops:
  7.2 98.3 %reduce-scatter.2.cloned.1.call-start = ((), (), s32[]{:S(2)}) async-start(), calls=%async_computation.1 | async-start | bytes 139264 | tf_op jit(solution)/shard_map/reduce_scatter | solution.py:97
  45.5 1.8 copy-start.3
  45.6 1.8 copy-start.4
  45.6 1.8 copy-start.5
  45.6 1.8 copy-start.6
  48.4 57.1 %copy-start.8 = (f32[8,1,256]{2,1,0:T(1,128)S(1)}, f32[8,1,256]{2,1,0:T(1,128)}, u32[]{:S(2)}) copy-start(f32[8,1,256]{2,1,0:T(1,128)} %param.21) | copy-start | bytes 24580
  48.4 57.8 %copy-start = (s32[2,256]{1,0:T(2,128)S(1)}, s32[2,256]{1,0:T(2,128)}, u32[]{:S(2)}) copy-start(s32[2,256]{1,0:T(2,128)} %param.24) | copy-start | bytes 6148
  48.4 57.8 %copy-start.1 = (bf16[2,8,16,256]{3,2,1,0:T(8,128)(2,1)S(1)}, bf16[2,8,16,256]{3,2,1,0:T(8,128)(2,1)}, u32[]{:S(2)}) copy-start(bf16[2,8,16,256]{3,2,1,0:T(8,128)(2,1)} %param.22) | copy-start | bytes 393220
  48.4 57.8 %copy-start.7 = (s32[3]{0:T(128)S(1)}, s32[3]{0:T(128)}, u32[]{:S(2)}) copy-start(s32[3]{0:T(128)} %constant.291.clone.1) | copy-start | bytes 40
  48.4 57.8 %copy-start.9 = (s32[32]{0:T(128)S(1)}, s32[32]{0:T(128)}, u32[]{:S(2)}) copy-start(s32[32]{0:T(128)} %param.25) | copy-start | bytes 388
  48.5 57.8 %copy-start.10 = (s32[32]{0:T(128)S(1)}, s32[32]{0:T(128)}, u32[]{:S(2)}) copy-start(s32[32]{0:T(128)} %param.27) | copy-start | bytes 388
  48.5 57.8 %copy-start.11 = (s32[32]{0:T(128)S(1)}, s32[32]{0:T(128)}, u32[]{:S(2)}) copy-start(s32[32]{0:T(128)} %param.26) | copy-start | bytes 388
  106.3 135.9 %all-reduce.2.cloned.1.call-start = ((), (), s32[]{:S(2)}) async-start(), calls=%async_computation.2 | async-start | bytes 131072 | tf_op jit(solution)/shard_map/while/body/eval_jaxpr/psum | solution.py:12
  482.8 119.7 %all-reduce.2.cloned.1.call-start = ((), (), s32[]{:S(2)}) async-start(), calls=%async_computation.2 | async-start | bytes 131072 | tf_op jit(solution)/shard_map/while/body/eval_jaxpr/psum | solution.py:12
  843.1 119.7 %all-reduce.2.cloned.1.call-start = ((), (), s32[]{:S(2)}) async-start(), calls=%async_computation.2 | async-start | bytes 131072 | tf_op jit(solution)/shard_map/while/body/eval_jaxpr/psum | solution.py:12
  1203.3 119.7 %all-reduce.2.cloned.1.call-start = ((), (), s32[]{:S(2)}) async-start(), calls=%async_computation.2 | async-start | bytes 131072 | tf_op jit(solution)/shard_map/while/body/eval_jaxpr/psum | solution.py:12
  1563.6 6.7 copy-start.2
Sparse Core Ops, SparseCore 0:
  48.5 56.9 reduce-scatter.1
  110.4 131.8 all-reduce.1
  486.8 115.5 all-reduce.1
  847.1 115.5 all-reduce.1
  1207.3 115.5 all-reduce.1
where the time goes:
time: 1580 us
  blocking collectives  884 us (56%)
  waiting for transfers between devices  502 us (32%)
  local copies, waits for them, and re-layouts  93.9 us (6%)
  other arithmetic  57.8 us (4%)
  loops' own time  25.7 us (2%)
    psum x8, blocking collectives, iterate(): gathered_sums = lax.psum(local_sums, ('bl', 'dir'))  854 us
    psum x4, waiting for transfers between devices, from_root(): return lax.psum(jnp.where(mine, shard, jnp.zeros_like(shard)), axis)  453 us
    reduce_scatter x1, waiting for transfers between devices, on_device(): lax.psum_scatter(partial_value, 'dir', scatter_dimension=1, tiled=True)  49.5 us
  transfers between devices with their start and end apart: 5, of which 5 were waited for; matrix products, arithmetic and copies ran while one was open for 2% of the time, Pallas kernels for 0%

commit v1 on v0

--- a/solution.py
+++ b/solution.py
@@ -5,11 +5,6 @@
 
 LM_ITERS = 2
 SOLVED = 4
-
-
-def from_root(shard, axis, root):
-    mine = lax.axis_index(axis) == root
-    return lax.psum(jnp.where(mine, shard, jnp.zeros_like(shard)), axis)
 
 
 def matrix_entry(mat, i, j):
@@ -80,21 +75,16 @@
     identity = jnp.zeros((8,), jnp.float32).at[0].set(1.0).at[6].set(1.0)
     start = lax.all_gather(gain_offsets, "bl", axis=2, tiled=True) + identity[None, :, None]
     groups = lax.axis_size("bl")
-    channels = visibilities.shape[1]
     total_channels = coherencies.shape[2]
-    owned_count = coherencies.shape[0]
     station_count = start.shape[2]
     damping_factor = visibilities.shape[2] * groups * total_channels / station_count
-    lane_index = lax.axis_index("dir")
+    coher_all = lax.all_to_all(coherencies, "dir", 2, 0, tiled=True)
     ends_p = jnp.take(start, stations[0], axis=2)
     ends_q = jnp.take(start, stations[1], axis=2)
-    owned_p = lax.dynamic_slice_in_dim(ends_p, lane_index * owned_count, owned_count, 0)
-    owned_q = lax.dynamic_slice_in_dim(ends_q, lane_index * owned_count, owned_count, 0)
-    gain_p = jnp.transpose(owned_p, (1, 0, 2))[:, :, None, :]
-    gain_q = jnp.transpose(owned_q, (1, 0, 2))[:, :, None, :]
-    coher_owned = jnp.transpose(coherencies, (1, 0, 2, 3)).astype(jnp.float32)
-    partial_value = jnp.sum(apply_gains(gain_p, coher_owned, gain_q), axis=1)
-    first_model = lax.psum_scatter(partial_value, "dir", scatter_dimension=1, tiled=True)
+    gain_p = jnp.transpose(ends_p, (1, 0, 2))[:, :, None, :]
+    gain_q = jnp.transpose(ends_q, (1, 0, 2))[:, :, None, :]
+    coher_f32 = jnp.transpose(coher_all, (1, 0, 2, 3)).astype(jnp.float32)
+    first_model = jnp.sum(apply_gains(gain_p, coher_f32, gain_q), axis=1)
     first_residual = visibilities - first_model
 
     def direction_model(gain_now, coher_now):
@@ -105,11 +95,9 @@
     def sweep(step_index, state):
         gain_table, residual = state
         which = solve_order[step_index]
-        owner_row = lax.dynamic_index_in_dim(coherencies, which % owned_count, 0, keepdims=False)
-        broadcast_rows = from_root(owner_row, "dir", which // owned_count)
-        coher_now = lax.dynamic_slice_in_dim(
-            broadcast_rows, lane_index * channels, channels, 1
-        ).astype(jnp.float32)
+        coher_now = lax.dynamic_index_in_dim(coher_all, which, 0, keepdims=False).astype(
+            jnp.float32
+        )
         damp_value = damping[which].astype(jnp.float32) * damping_factor
         gain_start = gain_table[which]
         target = residual + direction_model(gain_start, coher_now)
@@ -123,10 +111,10 @@
                 + jax.ops.segment_sum(second.T, stations[1], station_count)
             ).T
             gathered_sums = lax.psum(local_sums, ("bl", "dir"))
-            updated = solve_station(gathered_sums, gain_now, damp_value)
-            return jnp.where(round_index < counts[which], updated, gain_now)
+            return solve_station(gathered_sums, gain_now, damp_value)
 
-        gain_final = lax.fori_loop(0, LM_ITERS, iterate, gain_start)
+        rounds = jnp.clip(counts[which], 0, LM_ITERS)
+        gain_final = lax.fori_loop(0, rounds, iterate, gain_start)
         residual = target - direction_model(gain_final, coher_now)
         return (gain_table.at[which].set(gain_final), residual)
 

time: 1580 us -> 849 us (0.54)
  waiting for transfers between devices: 502 us -> 0.01 us
  blocking collectives: 884 us -> 730 us
  local copies, waits for them, and re-layouts: 93.9 us -> 49.5 us
  other arithmetic: 57.8 us -> 35.1 us
    psum x4 -> x0, waiting for transfers between devices: 453 us -> none  [from_root(): return lax.psum(jnp.where(mine, shard, jnp.zeros_like(shard)), axis)]
    psum x8 -> x7, blocking collectives: 854 us -> 703 us  [iterate(): gathered_sums = lax.psum(local_sums, ('bl', 'dir'))]
    reduce_scatter x1 -> x0, waiting for transfers between devices: 49.5 us -> none  [on_device(): lax.psum_scatter(partial_value, 'dir', scatter_dimension=1, tiled=True)]
    slice x153 -> x0, local copies, waits for them, and re-layouts: 25.3 us -> none  [matrix_entry(): return (mat[4 * i + 2 * j], mat[4 * i + 2 * j + 1])]
  transfers between devices with their start and end apart: 5 -> 1, of which waited for: 5 -> 0; matrix products, arithmetic and copies ran while one was open for 2% -> 1% of each run, Pallas kernels for 0% -> 0%
where the time goes in v1:
time: 849 us; the launch traced here: 847 us
  blocking collectives  730 us (86%)
  local copies, waits for them, and re-layouts  49.5 us (6%)
  other arithmetic  35.1 us (4%)
  starting transfers between devices  15.7 us (2%)
  loops' own time  15.4 us (2%)
    psum x7, blocking collectives, iterate(): gathered_sums = lax.psum(local_sums, ('bl', 'dir'))  703 us
    all_gather x1, blocking collectives, on_device(): lax.all_gather(gain_offsets, 'bl', axis=2, tiled=True)  27.2 us
  transfers between devices with their start and end apart: 1, of which 0 were waited for; matrix products, arithmetic and copies ran while one was open for 1% of the time, Pallas kernels for 0%

profile of v1, /device:TPU:1, one launch (start us, length us, event | category | flops | bytes accessed | tf_op | source)
XLA Modules:
  0.0 847.1 jit_solution(9811879134477437065)
XLA Ops:
  0.6 1.6 copy.1122
  2.2 15.7 %all-to-all-start = ((bf16[2,8,16,256]{3,1,0,2:T(8,128)(2,1)}), bf16[2,8,16,256]{3,1,0,2:T(8,128)(2,1)S(1)}, u32[]{:S(2)}, u32[]{:S(2)}) async-start(bf16[2,8,16,256]{3,1,0,2:T(8,128)(2,1)} %copy.1122), calls=%async_computation | async-start | bytes 262144 | tf_op jit(solution)/shard_map/all_to_all | solution.py:81
  19.7 27.2 %all_gather.3 = f32[32,8,512]{0,1,2:T(8,128)S(1)} all-gather(f32[32,8,16]{0,1,2:T(8,128)S(1)} %copy.1120), channel_id=1, replica_groups=mesh['bl'=32,'dir'=16] {'bl'}, dimensions={2}, use_global_device_ids=true | all-gather | bytes 540672 | tf_op jit(solution)/shard_map/all_gather | solution.py:76
  48.0 2.0 gather_fusion.7
  50.0 1.6 copy.1124
  51.6 2.0 gather_fusion.6
  53.6 1.6 copy.1121
  57.4 788.4 %while.42 = (s32[]{:T(128)}, f32[32,8,512]{2,1,0:T(8,128)S(1)}, f32[8,1,256]{2,1,0:T(1,128)S(1)}, s32[32]{0:T(128)S(1)}, s32[32]{0:T(128)S(1)}, /*index=5*/bf16[...) while((s32[]{:T(128)}, f32[32,8,512]{2,1,0:T(8,128)S(1)}, ...), condition=%wide.region_8.12_spmd, body=%wide.region_1.11_spmd.sunk | while | flops 253464 | bytes 1958014 | solution.py:121
  64.8 215.9 %while.43 = (s32[]{:T(128)}, f32[8,512]{1,0:T(8,128)S(1)}, s32[]{:T(128)}, s32[2,256]{1,0:T(2,128)S(1)}, f32[8,1,256]{2,1,0:T(1,128)S(1)}, /*index=5*/f32[8,1,25...) while((s32[]{:T(128)}, f32[8,512]{1,0:T(8,128)S(1)}, ...), condition=%wide.region_7.10_spmd, body=%wide.region_3.9_spmd.sunk | while | flops 160768 | bytes 1263793 | solution.py:117
  67.0 1.5 scatter_custom_fusion.11
  69.0 1.5 scatter_custom_fusion.10
  70.6 103.1 %psum.9 = f32[12,512]{1,0:T(8,128)S(1)} all-reduce(f32[12,512]{1,0:T(8,128)S(1)} %add_bitcast_fusion.2), channel_id=1, replica_groups=mesh['bl'=32,'dir'=16] {'bl','dir'}, use_global_device_ids=true, to_apply=%region_6.8 | all-reduce | flops 6144 | bytes 49152 | tf_op jit(solution)/shard_map/while/body/eval_jaxpr/while/body/psum | solution.py:113
  179.8 100.7 %psum.9 = f32[12,512]{1,0:T(8,128)S(1)} all-reduce(f32[12,512]{1,0:T(8,128)S(1)} %add_bitcast_fusion.2), channel_id=1, replica_groups=mesh['bl'=32,'dir'=16] {'bl','dir'}, use_global_device_ids=true, to_apply=%region_6.8 | all-reduce | flops 6144 | bytes 49152 | tf_op jit(solution)/shard_map/while/body/eval_jaxpr/while/body/psum | solution.py:113
  291.4 211.9 %while.43 = (s32[]{:T(128)}, f32[8,512]{1,0:T(8,128)S(1)}, s32[]{:T(128)}, s32[2,256]{1,0:T(2,128)S(1)}, f32[8,1,256]{2,1,0:T(1,128)S(1)}, /*index=5*/f32[8,1,25...) while((s32[]{:T(128)}, f32[8,512]{1,0:T(8,128)S(1)}, ...), condition=%wide.region_7.10_spmd, body=%wide.region_3.9_spmd.sunk | while | flops 160768 | bytes 1263793 | solution.py:117
  293.6 1.5 scatter_custom_fusion.11
  295.5 1.5 scatter_custom_fusion.10
  297.2 99.4 %psum.9 = f32[12,512]{1,0:T(8,128)S(1)} all-reduce(f32[12,512]{1,0:T(8,128)S(1)} %add_bitcast_fusion.2), channel_id=1, replica_groups=mesh['bl'=32,'dir'=16] {'bl','dir'}, use_global_device_ids=true, to_apply=%region_6.8 | all-reduce | flops 6144 | bytes 49152 | tf_op jit(solution)/shard_map/while/body/eval_jaxpr/while/body/psum | solution.py:113
  399.1 1.5 scatter_custom_fusion.11
  402.7 100.4 %psum.9 = f32[12,512]{1,0:T(8,128)S(1)} all-reduce(f32[12,512]{1,0:T(8,128)S(1)} %add_bitcast_fusion.2), channel_id=1, replica_groups=mesh['bl'=32,'dir'=16] {'bl','dir'}, use_global_device_ids=true, to_apply=%region_6.8 | all-reduce | flops 6144 | bytes 49152 | tf_op jit(solution)/shard_map/while/body/eval_jaxpr/while/body/psum | solution.py:113
  513.9 105.7 %while.43 = (s32[]{:T(128)}, f32[8,512]{1,0:T(8,128)S(1)}, s32[]{:T(128)}, s32[2,256]{1,0:T(2,128)S(1)}, f32[8,1,256]{2,1,0:T(1,128)S(1)}, /*index=5*/f32[8,1,25...) while((s32[]{:T(128)}, f32[8,512]{1,0:T(8,128)S(1)}, ...), condition=%wide.region_7.10_spmd, body=%wide.region_3.9_spmd.sunk | while | flops 160768 | bytes 1263793 | solution.py:117
  519.7 99.6 %psum.9 = f32[12,512]{1,0:T(8,128)S(1)} all-reduce(f32[12,512]{1,0:T(8,128)S(1)} %add_bitcast_fusion.2), channel_id=1, replica_groups=mesh['bl'=32,'dir'=16] {'bl','dir'}, use_global_device_ids=true, to_apply=%region_6.8 | all-reduce | flops 6144 | bytes 49152 | tf_op jit(solution)/shard_map/while/body/eval_jaxpr/while/body/psum | solution.py:113
  630.2 212.1 %while.43 = (s32[]{:T(128)}, f32[8,512]{1,0:T(8,128)S(1)}, s32[]{:T(128)}, s32[2,256]{1,0:T(2,128)S(1)}, f32[8,1,256]{2,1,0:T(1,128)S(1)}, /*index=5*/f32[8,1,25...) while((s32[]{:T(128)}, f32[8,512]{1,0:T(8,128)S(1)}, ...), condition=%wide.region_7.10_spmd, body=%wide.region_3.9_spmd.sunk | while | flops 160768 | bytes 1263793 | solution.py:117
  636.0 100.5 %psum.9 = f32[12,512]{1,0:T(8,128)S(1)} all-reduce(f32[12,512]{1,0:T(8,128)S(1)} %add_bitcast_fusion.2), channel_id=1, replica_groups=mesh['bl'=32,'dir'=16] {'bl','dir'}, use_global_device_ids=true, to_apply=%region_6.8 | all-reduce | flops 6144 | bytes 49152 | tf_op jit(solution)/shard_map/while/body/eval_jaxpr/while/body/psum | solution.py:113
  742.5 99.6 %psum.9 = f32[12,512]{1,0:T(8,128)S(1)} all-reduce(f32[12,512]{1,0:T(8,128)S(1)} %add_bitcast_fusion.2), channel_id=1, replica_groups=mesh['bl'=32,'dir'=16] {'bl','dir'}, use_global_device_ids=true, to_apply=%region_6.8 | all-reduce | flops 6144 | bytes 49152 | tf_op jit(solution)/shard_map/while/body/eval_jaxpr/while/body/psum | solution.py:113
  (603 shorter events, 68.3 us)
Async XLA Ops:
  0.6 46.2 %copy-start.4 = (f32[8]{0:T(128)S(1)}, f32[8]{0:T(128)}, u32[]{:S(2)}) copy-start(f32[8]{0:T(128)} %constant.188.clone.1) | copy-start | bytes 100
  2.2 53.1 %all-to-all-start = ((bf16[2,8,16,256]{3,1,0,2:T(8,128)(2,1)}), bf16[2,8,16,256]{3,1,0,2:T(8,128)(2,1)S(1)}, u32[]{:S(2)}, u32[]{:S(2)}) async-start(bf16[2,8,16,256]{3,1,0,2:T(8,128)(2,1)} %copy.1122), calls=%async_computation | async-start | bytes 262144 | tf_op jit(solution)/shard_map/all_to_all | solution.py:81
  55.2 2.1 copy-start.3
  55.2 2.1 copy-start
  55.3 2.1 copy-start.2
  55.3 2.1 copy-start.5
  55.3 2.1 copy-start.6
  55.3 2.1 copy-start.7
  845.8 1.3 copy-start.1

commit v2 on v1

--- a/solution.py
+++ b/solution.py
@@ -1,7 +1,13 @@
+import functools
+
 import jax
 import jax.numpy as jnp
 from jax import lax
 from jax.sharding import PartitionSpec as P
+from jax.experimental import pallas as pl
+from jax.experimental.pallas import tpu as pltpu
+
+MESH_ID = pl.DeviceIdType.MESH
 
 LM_ITERS = 2
 SOLVED = 4
@@ -71,10 +77,90 @@
     return matmul_two(numerator, inverse)
 
 
+def all_reduce_kernel(nz, nb, x_ref, o_ref, r1, r2, r3, s1, q1, s2, q2, s3, q3):
+    mz = lax.axis_index("dir")
+    mb = lax.axis_index("bl")
+    z_peers = [lax.rem(mz + k, nz) for k in range(1, nz)]
+    b_peers = [lax.rem(mb + k, nb) for k in range(1, nb)]
+
+    barrier = pltpu.get_barrier_semaphore()
+    for p in z_peers:
+        pl.semaphore_signal(barrier, 1, device_id=(mb, p), device_id_type=MESH_ID)
+    for p in b_peers:
+        pl.semaphore_signal(barrier, 1, device_id=(p, mz), device_id_type=MESH_ID)
+    pl.semaphore_wait(barrier, (nz - 1) + (nb - 1))
+
+    def exchange(peers, src_of, buf, me, send_sems, recv_sems, device_of):
+        sent = []
+        for p in peers:
+            c = pltpu.make_async_remote_copy(
+                src_ref=src_of(p),
+                dst_ref=buf.at[me],
+                send_sem=send_sems.at[p],
+                recv_sem=recv_sems.at[me],
+                device_id=device_of(p),
+                device_id_type=MESH_ID,
+            )
+            c.start()
+            sent.append(c)
+        for p in peers:
+            pltpu.make_async_remote_copy(
+                src_ref=buf.at[p],
+                dst_ref=buf.at[p],
+                send_sem=send_sems.at[p],
+                recv_sem=recv_sems.at[p],
+                device_id=device_of(p),
+                device_id_type=MESH_ID,
+            ).wait_recv()
+        for c in sent:
+            c.wait_send()
+
+    exchange(z_peers, lambda p: x_ref.at[p], r1, mz, s1, q1, lambda p: (mb, p))
+    own = x_ref[mz]
+    for p in z_peers:
+        own = own + r1[p]
+    r2[mb] = own
+    exchange(b_peers, lambda p: r2.at[mb], r2, mb, s2, q2, lambda p: (p, mz))
+    total = r2[mb]
+    for p in b_peers:
+        total = total + r2[p]
+    r3[mz] = total
+    exchange(z_peers, lambda p: r3.at[mz], r3, mz, s3, q3, lambda p: (mb, p))
+    o_ref[...] = r3[...]
+
+
+def all_reduce(payload, nz, nb):
+    chunk_shape = payload.shape[1:]
+    return pl.pallas_call(
+        functools.partial(all_reduce_kernel, nz, nb),
+        out_shape=jax.ShapeDtypeStruct(payload.shape, payload.dtype),
+        in_specs=[pl.BlockSpec(memory_space=pltpu.VMEM)],
+        out_specs=pl.BlockSpec(memory_space=pltpu.VMEM),
+        scratch_shapes=[
+            pltpu.VMEM((nz,) + chunk_shape, payload.dtype),
+            pltpu.VMEM((nb,) + chunk_shape, payload.dtype),
+            pltpu.VMEM((nz,) + chunk_shape, payload.dtype),
+            pltpu.SemaphoreType.DMA((nz,)),
+            pltpu.SemaphoreType.DMA((nz,)),
+            pltpu.SemaphoreType.DMA((nb,)),
+            pltpu.SemaphoreType.DMA((nb,)),
+            pltpu.SemaphoreType.DMA((nz,)),
+            pltpu.SemaphoreType.DMA((nz,)),
+        ],
+        compiler_params=pltpu.CompilerParams(collective_id=0, has_side_effects=True),
+    )(payload)
+
+
+def station_sum(rows, nz, nb):
+    flat = rows.reshape(nz, -1, 128)
+    return all_reduce(flat, nz, nb).reshape(rows.shape)
+
+
 def on_device(visibilities, coherencies, gain_offsets, stations, solve_order, counts, damping):
     identity = jnp.zeros((8,), jnp.float32).at[0].set(1.0).at[6].set(1.0)
     start = lax.all_gather(gain_offsets, "bl", axis=2, tiled=True) + identity[None, :, None]
     groups = lax.axis_size("bl")
+    nz = lax.axis_size("dir")
     total_channels = coherencies.shape[2]
     station_count = start.shape[2]
     damping_factor = visibilities.shape[2] * groups * total_channels / station_count
@@ -106,11 +192,10 @@
             gain_p = jnp.take(gain_now, stations[0], axis=1)[:, None, :]
             gain_q = jnp.take(gain_now, stations[1], axis=1)[:, None, :]
             leading_endpoint, second = station_terms(gain_p, gain_q, coher_now, target)
-            local_sums = (
-                jax.ops.segment_sum(leading_endpoint.T, stations[0], station_count)
-                + jax.ops.segment_sum(second.T, stations[1], station_count)
-            ).T
-            gathered_sums = lax.psum(local_sums, ("bl", "dir"))
+            local_rows = jax.ops.segment_sum(
+                leading_endpoint.T, stations[0], station_count
+            ) + jax.ops.segment_sum(second.T, stations[1], station_count)
+            gathered_sums = station_sum(local_rows, nz, groups).T
             return solve_station(gathered_sums, gain_now, damp_value)
 
         rounds = jnp.clip(counts[which], 0, LM_ITERS)

time: 849 us -> 357 us (0.42)
  blocking collectives: 730 us -> 27.2 us
  Pallas kernels: 0 us -> 200 us
  local copies, waits for them, and re-layouts: 49.5 us -> 61.2 us
    psum x7 -> x0, blocking collectives: 703 us -> none  [iterate(): gathered_sums = lax.psum(local_sums, ('bl', 'dir'))]
    pallas_call x0 -> x7, Pallas kernels: none -> 200 us  [all_reduce(): pl.pallas_call(functools.partial(all_reduce_kernel, nz, nb), out_shape=ja...]
    reshape x0 -> x21, local copies, waits for them, and re-layouts: none -> 13.5 us  [the longest x14 7.99 us: station_sum(): return all_reduce(flat, nz, nb).reshape(rows.shape)]
  transfers between devices with their start and end apart: 1 -> 1, of which waited for: 0 -> 0; matrix products, arithmetic and copies ran while one was open for 1% -> 3% of each run, Pallas kernels for 0% -> 0%
where the time goes in v2:
time: 357 us; the launch traced here: 356 us
  Pallas kernels  200 us (56%)
  local copies, waits for them, and re-layouts  61.2 us (17%)
  other arithmetic  34.8 us (10%)
  blocking collectives  27.2 us (8%)
  starting transfers between devices  15.7 us (4%)
  loops' own time  15.6 us (4%)
    pallas_call x7, Pallas kernels, all_reduce(): pl.pallas_call(functools.partial(all_reduce_kernel, nz, nb), out_shape=ja...  200 us
    all_gather x1, blocking collectives, on_device(): lax.all_gather(gain_offsets, 'bl', axis=2, tiled=True)  27.2 us
    all_to_all x1, starting transfers between devices, on_device(): coher_all = lax.all_to_all(coherencies, 'dir', 2, 0, tiled=True)  15.7 us
    another operation x1, loops' own time, on_device(): lax.fori_loop(0, SOLVED, sweep, (start, first_residual))  14 us
    scatter-add x7, other arithmetic, iterate(): jax.ops.segment_sum(leading_endpoint.T, stations[0], station_count)  10.5 us
    scatter-add x7, other arithmetic, iterate(): jax.ops.segment_sum(second.T, stations[1], station_count)  10.5 us
    reshape x14, local copies, waits for them, and re-layouts, station_sum(): return all_reduce(flat, nz, nb).reshape(rows.shape)  7.99 us
  transfers between devices with their start and end apart: 1, of which 0 were waited for; matrix products, arithmetic and copies ran while one was open for 3% of the time, Pallas kernels for 0%

profile of v2, /device:TPU:1, one launch (start us, length us, event | category | flops | bytes accessed | tf_op | source)
XLA Modules:
  0.0 355.6 jit_solution(12859835635304709835)
XLA Ops:
  0.6 1.6 copy.1121
  2.2 15.7 %all-to-all-start = ((bf16[2,8,16,256]{3,1,0,2:T(8,128)(2,1)}), bf16[2,8,16,256]{3,1,0,2:T(8,128)(2,1)S(1)}, u32[]{:S(2)}, u32[]{:S(2)}) async-start(bf16[2,8,16,256]{3,1,0,2:T(8,128)(2,1)} %copy.1121), calls=%async_computation | async-start | bytes 262144 | tf_op jit(solution)/shard_map/all_to_all | solution.py:167
  19.7 27.2 %all_gather.3 = f32[32,8,512]{0,1,2:T(8,128)S(1)} all-gather(f32[32,8,16]{0,1,2:T(8,128)S(1)} %copy.1119), channel_id=1, replica_groups=mesh['bl'=32,'dir'=16] {'bl'}, dimensions={2}, use_global_device_ids=true | all-gather | bytes 540672 | tf_op jit(solution)/shard_map/all_gather | solution.py:161
  48.0 2.0 gather_fusion.7
  50.0 1.6 copy.1123
  51.6 2.0 gather_fusion.6
  53.6 1.6 copy.1120
  57.4 296.8 %while.42 = (s32[]{:T(128)}, f32[32,8,512]{2,1,0:T(8,128)S(1)}, f32[8,1,256]{2,1,0:T(1,128)S(1)}, s32[32]{0:T(128)S(1)}, s32[32]{0:T(128)S(1)}, /*index=5*/bf16[...) while((s32[]{:T(128)}, f32[32,8,512]{2,1,0:T(8,128)S(1)}, ...), condition=%wide.region_7.11_spmd, body=%wide.region_1.10_spmd.sunk | while | flops 247320 | bytes 1958014 | solution.py:206
  64.8 40.2 %while.43 = (s32[]{:T(128)}, f32[8,512]{1,0:T(8,128)S(1)}, s32[]{:T(128)}, s32[2,256]{1,0:T(2,128)S(1)}, f32[8,1,256]{2,1,0:T(1,128)S(1)}, /*index=5*/f32[8,1,25...) while((s32[]{:T(128)}, f32[8,512]{1,0:T(8,128)S(1)}, ...), condition=%wide.region_6.9_spmd, body=%wide.region_3.8_spmd.sunk | while | flops 154624 | bytes 1263793 | solution.py:202
  67.0 1.5 scatter_custom_fusion.11
  68.8 1.5 scatter_custom_fusion.10
  71.1 32.4 %body.2 = f32[16,3,128]{2,1,0:T(4,128)} custom-call(f32[16,3,128]{2,1,0:T(4,128)} %reshape.1420.x_ref), custom_call_target="tpu_custom_call" | custom-call | tf_op jit(solution)/shard_map/while/body/eval_jaxpr/while/body/pallas_call | solution.py:134
  115.4 72.3 %while.43 = (s32[]{:T(128)}, f32[8,512]{1,0:T(8,128)S(1)}, s32[]{:T(128)}, s32[2,256]{1,0:T(2,128)S(1)}, f32[8,1,256]{2,1,0:T(1,128)S(1)}, /*index=5*/f32[8,1,25...) while((s32[]{:T(128)}, f32[8,512]{1,0:T(8,128)S(1)}, ...), condition=%wide.region_6.9_spmd, body=%wide.region_3.8_spmd.sunk | while | flops 154624 | bytes 1263793 | solution.py:202
  117.7 1.5 scatter_custom_fusion.11
  119.5 1.5 scatter_custom_fusion.10
  121.8 25.9 %body.2 = f32[16,3,128]{2,1,0:T(4,128)} custom-call(f32[16,3,128]{2,1,0:T(4,128)} %reshape.1420.x_ref), custom_call_target="tpu_custom_call" | custom-call | tf_op jit(solution)/shard_map/while/body/eval_jaxpr/while/body/pallas_call | solution.py:134
  153.2 1.5 scatter_custom_fusion.10
  155.5 30.8 %body.2 = f32[16,3,128]{2,1,0:T(4,128)} custom-call(f32[16,3,128]{2,1,0:T(4,128)} %reshape.1420.x_ref), custom_call_target="tpu_custom_call" | custom-call | tf_op jit(solution)/shard_map/while/body/eval_jaxpr/while/body/pallas_call | solution.py:134
  198.2 71.0 %while.43 = (s32[]{:T(128)}, f32[8,512]{1,0:T(8,128)S(1)}, s32[]{:T(128)}, s32[2,256]{1,0:T(2,128)S(1)}, f32[8,1,256]{2,1,0:T(1,128)S(1)}, /*index=5*/f32[8,1,25...) while((s32[]{:T(128)}, f32[8,512]{1,0:T(8,128)S(1)}, ...), condition=%wide.region_6.9_spmd, body=%wide.region_3.8_spmd.sunk | while | flops 154624 | bytes 1263793 | solution.py:202
  204.6 25.2 %body.2 = f32[16,3,128]{2,1,0:T(4,128)} custom-call(f32[16,3,128]{2,1,0:T(4,128)} %reshape.1420.x_ref), custom_call_target="tpu_custom_call" | custom-call | tf_op jit(solution)/shard_map/while/body/eval_jaxpr/while/body/pallas_call | solution.py:134
  237.6 30.2 %body.2 = f32[16,3,128]{2,1,0:T(4,128)} custom-call(f32[16,3,128]{2,1,0:T(4,128)} %reshape.1420.x_ref), custom_call_target="tpu_custom_call" | custom-call | tf_op jit(solution)/shard_map/while/body/eval_jaxpr/while/body/pallas_call | solution.py:134
  279.6 71.3 %while.43 = (s32[]{:T(128)}, f32[8,512]{1,0:T(8,128)S(1)}, s32[]{:T(128)}, s32[2,256]{1,0:T(2,128)S(1)}, f32[8,1,256]{2,1,0:T(1,128)S(1)}, /*index=5*/f32[8,1,25...) while((s32[]{:T(128)}, f32[8,512]{1,0:T(8,128)S(1)}, ...), condition=%wide.region_6.9_spmd, body=%wide.region_3.8_spmd.sunk | while | flops 154624 | bytes 1263793 | solution.py:202
  286.0 26.0 %body.2 = f32[16,3,128]{2,1,0:T(4,128)} custom-call(f32[16,3,128]{2,1,0:T(4,128)} %reshape.1420.x_ref), custom_call_target="tpu_custom_call" | custom-call | tf_op jit(solution)/shard_map/while/body/eval_jaxpr/while/body/pallas_call | solution.py:134
  319.8 29.7 %body.2 = f32[16,3,128]{2,1,0:T(4,128)} custom-call(f32[16,3,128]{2,1,0:T(4,128)} %reshape.1420.x_ref), custom_call_target="tpu_custom_call" | custom-call | tf_op jit(solution)/shard_map/while/body/eval_jaxpr/while/body/pallas_call | solution.py:134
  (610 shorter events, 79.7 us)
Async XLA Ops:
  0.6 46.2 %copy-start.4 = (f32[8]{0:T(128)S(1)}, f32[8]{0:T(128)}, u32[]{:S(2)}) copy-start(f32[8]{0:T(128)} %constant.188.clone.1) | copy-start | bytes 100
  2.2 53.1 %all-to-all-start = ((bf16[2,8,16,256]{3,1,0,2:T(8,128)(2,1)}), bf16[2,8,16,256]{3,1,0,2:T(8,128)(2,1)S(1)}, u32[]{:S(2)}, u32[]{:S(2)}) async-start(bf16[2,8,16,256]{3,1,0,2:T(8,128)(2,1)} %copy.1121), calls=%async_computation | async-start | bytes 262144 | tf_op jit(solution)/shard_map/all_to_all | solution.py:167
  55.2 2.1 copy-start.3
  55.3 2.1 copy-start
  55.3 2.1 copy-start.2
  55.3 2.1 copy-start.5
  55.3 2.1 copy-start.6
  55.3 2.1 copy-start.7
  354.3 1.3 copy-start.1

commit v3 on v2

--- a/solution.py
+++ b/solution.py
@@ -77,17 +77,17 @@
     return matmul_two(numerator, inverse)
 
 
-def all_reduce_kernel(nz, nb, x_ref, o_ref, r1, r2, r3, s1, q1, s2, q2, s3, q3):
+def all_reduce_kernel(nb, nz, x_ref, o_ref, r1, r2, r3, s1, q1, s2, q2, s3, q3):
     mz = lax.axis_index("dir")
     mb = lax.axis_index("bl")
     z_peers = [lax.rem(mz + k, nz) for k in range(1, nz)]
     b_peers = [lax.rem(mb + k, nb) for k in range(1, nb)]
 
     barrier = pltpu.get_barrier_semaphore()
+    for p in b_peers:
+        pl.semaphore_signal(barrier, 1, device_id=(p, mz), device_id_type=MESH_ID)
     for p in z_peers:
         pl.semaphore_signal(barrier, 1, device_id=(mb, p), device_id_type=MESH_ID)
-    for p in b_peers:
-        pl.semaphore_signal(barrier, 1, device_id=(p, mz), device_id_type=MESH_ID)
     pl.semaphore_wait(barrier, (nz - 1) + (nb - 1))
 
     def exchange(peers, src_of, buf, me, send_sems, recv_sems, device_of):
@@ -115,45 +115,47 @@
         for c in sent:
             c.wait_send()
 
-    exchange(z_peers, lambda p: x_ref.at[p], r1, mz, s1, q1, lambda p: (mb, p))
-    own = x_ref[mz]
+    exchange(b_peers, lambda p: x_ref.at[p], r1, mb, s1, q1, lambda p: (p, mz))
+    own = x_ref[mb]
+    for p in b_peers:
+        own = own + r1[p]
+    r2[mz] = own
+    exchange(z_peers, lambda p: r2.at[mz], r2, mz, s2, q2, lambda p: (mb, p))
+    total = r2[mz]
     for p in z_peers:
-        own = own + r1[p]
-    r2[mb] = own
-    exchange(b_peers, lambda p: r2.at[mb], r2, mb, s2, q2, lambda p: (p, mz))
-    total = r2[mb]
-    for p in b_peers:
         total = total + r2[p]
-    r3[mz] = total
-    exchange(z_peers, lambda p: r3.at[mz], r3, mz, s3, q3, lambda p: (mb, p))
+    r3[mb] = total
+    exchange(b_peers, lambda p: r3.at[mb], r3, mb, s3, q3, lambda p: (p, mz))
     o_ref[...] = r3[...]
 
 
-def all_reduce(payload, nz, nb):
+def all_reduce(payload, nb, nz):
     chunk_shape = payload.shape[1:]
     return pl.pallas_call(
-        functools.partial(all_reduce_kernel, nz, nb),
+        functools.partial(all_reduce_kernel, nb, nz),
         out_shape=jax.ShapeDtypeStruct(payload.shape, payload.dtype),
         in_specs=[pl.BlockSpec(memory_space=pltpu.VMEM)],
         out_specs=pl.BlockSpec(memory_space=pltpu.VMEM),
         scratch_shapes=[
+            pltpu.VMEM((nb,) + chunk_shape, payload.dtype),
             pltpu.VMEM((nz,) + chunk_shape, payload.dtype),
             pltpu.VMEM((nb,) + chunk_shape, payload.dtype),
-            pltpu.VMEM((nz,) + chunk_shape, payload.dtype),
+            pltpu.SemaphoreType.DMA((nb,)),
+            pltpu.SemaphoreType.DMA((nb,)),
             pltpu.SemaphoreType.DMA((nz,)),
             pltpu.SemaphoreType.DMA((nz,)),
             pltpu.SemaphoreType.DMA((nb,)),
             pltpu.SemaphoreType.DMA((nb,)),
-            pltpu.SemaphoreType.DMA((nz,)),
-            pltpu.SemaphoreType.DMA((nz,)),
         ],
         compiler_params=pltpu.CompilerParams(collective_id=0, has_side_effects=True),
     )(payload)
 
 
 def station_sum(rows, nz, nb):
-    flat = rows.reshape(nz, -1, 128)
-    return all_reduce(flat, nz, nb).reshape(rows.shape)
+    width = rows.shape[0] * 16
+    padded = jnp.pad(rows, ((0, 0), (0, 16 - rows.shape[1])))
+    summed = all_reduce(padded.reshape(nb, width // (nb * 128), 128), nb, nz)
+    return summed.reshape(rows.shape[0], 16)[:, : rows.shape[1]]
 
 
 def on_device(visibilities, coherencies, gain_offsets, stations, solve_order, counts, damping):

time: 357 us -> 272 us (0.76)
  Pallas kernels: 200 us -> 132 us
  local copies, waits for them, and re-layouts: 61.2 us -> 52.6 us
  other arithmetic: 34.8 us -> 27.5 us
    pallas_call x7 -> x5, Pallas kernels: 200 us -> 132 us  [all_reduce(): pl.pallas_call(functools.partial(all_reduce_kernel, nb, nz), out_shape=ja...]
    reshape x21 -> x10, local copies, waits for them, and re-layouts: 13.5 us -> 8.28 us  [the longest x5 4.51 us: station_sum(): return summed.reshape(rows.shape[0], 16)[:, :rows.shape[1]]]
    scatter-add x7 -> x5, other arithmetic: 10.5 us -> 7.47 us  [iterate(): jax.ops.segment_sum(leading_endpoint.T, stations[0], station_count)]
    scatter-add x7 -> x5, other arithmetic: 10.5 us -> 7.47 us  [iterate(): jax.ops.segment_sum(second.T, stations[1], station_count)]
  transfers between devices with their start and end apart: 1 -> 1, of which waited for: 0 -> 0; matrix products, arithmetic and copies ran while one was open for 3% -> 4% of each run, Pallas kernels for 0% -> 0%
where the time goes in v3:
time: 272 us; the launch traced here: 271 us
  Pallas kernels  132 us (49%)
  local copies, waits for them, and re-layouts  52.6 us (19%)
  other arithmetic  27.5 us (10%)
  blocking collectives  27.2 us (10%)
  starting transfers between devices  15.7 us (6%)
  loops' own time  15.2 us (6%)
    pallas_call x5, Pallas kernels, all_reduce(): pl.pallas_call(functools.partial(all_reduce_kernel, nb, nz), out_shape=ja...  132 us
    all_gather x1, blocking collectives, on_device(): lax.all_gather(gain_offsets, 'bl', axis=2, tiled=True)  27.2 us
    all_to_all x1, starting transfers between devices, on_device(): coher_all = lax.all_to_all(coherencies, 'dir', 2, 0, tiled=True)  15.7 us
    another operation x1, loops' own time, on_device(): lax.fori_loop(0, SOLVED, sweep, (start, first_residual))  14 us
    scatter-add x5, other arithmetic, iterate(): jax.ops.segment_sum(second.T, stations[1], station_count)  7.47 us
    scatter-add x5, other arithmetic, iterate(): jax.ops.segment_sum(leading_endpoint.T, stations[0], station_count)  7.47 us
    gather x16, local copies, waits for them, and re-layouts, direction_model(): gain_p = jnp.take(gain_now, stations[0], axis=1)[:, None, :]  6.35 us
    gather x16, local copies, waits for them, and re-layouts, direction_model(): gain_q = jnp.take(gain_now, stations[1], axis=1)[:, None, :]  6.31 us
  transfers between devices with their start and end apart: 1, of which 0 were waited for; matrix products, arithmetic and copies ran while one was open for 4% of the time, Pallas kernels for 0%

profile of v3, /device:TPU:1, one launch (start us, length us, event | category | flops | bytes accessed | tf_op | source)
XLA Modules:
  0.0 270.7 jit_solution(10872243162661369460)
XLA Ops:
  0.6 1.6 copy.1121
  2.2 15.7 %all-to-all-start = ((bf16[2,8,16,256]{3,1,0,2:T(8,128)(2,1)}), bf16[2,8,16,256]{3,1,0,2:T(8,128)(2,1)S(1)}, u32[]{:S(2)}, u32[]{:S(2)}) async-start(bf16[2,8,16,256]{3,1,0,2:T(8,128)(2,1)} %copy.1121), calls=%async_computation | async-start | bytes 262144 | tf_op jit(solution)/shard_map/all_to_all | solution.py:169
  19.7 27.2 %all_gather.3 = f32[32,8,512]{0,1,2:T(8,128)S(1)} all-gather(f32[32,8,16]{0,1,2:T(8,128)S(1)} %copy.1119), channel_id=1, replica_groups=mesh['bl'=32,'dir'=16] {'bl'}, dimensions={2}, use_global_device_ids=true | all-gather | bytes 540672 | tf_op jit(solution)/shard_map/all_gather | solution.py:163
  48.0 2.0 gather_fusion.7
  50.0 1.6 copy.1123
  51.6 2.0 gather_fusion.6
  53.6 1.6 copy.1120
  57.4 212.0 %while.52 = (s32[]{:T(128)}, f32[32,8,512]{2,1,0:T(8,128)S(1)}, f32[8,1,256]{2,1,0:T(1,128)S(1)}, s32[32]{0:T(128)S(1)}, s32[32]{0:T(128)S(1)}, /*index=5*/bf16[...) while((s32[]{:T(128)}, f32[32,8,512]{2,1,0:T(8,128)S(1)}, ...), condition=%wide.region_7.11_spmd, body=%wide.region_1.10_spmd.sunk | while | flops 247320 | bytes 2048130 | solution.py:208
  64.8 36.1 %while.53 = (s32[]{:T(128)}, f32[8,512]{1,0:T(8,128)S(1)}, s32[]{:T(128)}, s32[2,256]{1,0:T(2,128)S(1)}, f32[8,1,256]{2,1,0:T(1,128)S(1)}, /*index=5*/f32[8,1,25...) while((s32[]{:T(128)}, f32[8,512]{1,0:T(8,128)S(1)}, ...), condition=%wide.region_6.9_spmd, body=%wide.region_3.8_spmd.sunk | while | flops 154624 | bytes 1353909 | solution.py:204
  67.0 1.5 scatter_custom_fusion.11
  68.8 1.5 scatter_custom_fusion.10
  71.1 28.4 %body.4 = f32[32,2,128]{2,1,0:T(2,128)} custom-call(f32[32,2,128]{2,1,0:T(2,128)} %reshape.1467.x_ref), custom_call_target="tpu_custom_call" | custom-call | tf_op jit(solution)/shard_map/while/body/eval_jaxpr/while/body/pallas_call | solution.py:134
  111.3 66.9 %while.53 = (s32[]{:T(128)}, f32[8,512]{1,0:T(8,128)S(1)}, s32[]{:T(128)}, s32[2,256]{1,0:T(2,128)S(1)}, f32[8,1,256]{2,1,0:T(1,128)S(1)}, /*index=5*/f32[8,1,25...) while((s32[]{:T(128)}, f32[8,512]{1,0:T(8,128)S(1)}, ...), condition=%wide.region_6.9_spmd, body=%wide.region_3.8_spmd.sunk | while | flops 154624 | bytes 1353909 | solution.py:204
  113.5 1.5 scatter_custom_fusion.11
  117.7 25.7 %body.4 = f32[32,2,128]{2,1,0:T(2,128)} custom-call(f32[32,2,128]{2,1,0:T(2,128)} %reshape.1467.x_ref), custom_call_target="tpu_custom_call" | custom-call | tf_op jit(solution)/shard_map/while/body/eval_jaxpr/while/body/pallas_call | solution.py:134
  146.9 1.5 scatter_custom_fusion.11
  148.7 1.5 scatter_custom_fusion.10
  151.0 25.9 %body.4 = f32[32,2,128]{2,1,0:T(2,128)} custom-call(f32[32,2,128]{2,1,0:T(2,128)} %reshape.1467.x_ref), custom_call_target="tpu_custom_call" | custom-call | tf_op jit(solution)/shard_map/while/body/eval_jaxpr/while/body/pallas_call | solution.py:134
  188.7 33.5 %while.53 = (s32[]{:T(128)}, f32[8,512]{1,0:T(8,128)S(1)}, s32[]{:T(128)}, s32[2,256]{1,0:T(2,128)S(1)}, f32[8,1,256]{2,1,0:T(1,128)S(1)}, /*index=5*/f32[8,1,25...) while((s32[]{:T(128)}, f32[8,512]{1,0:T(8,128)S(1)}, ...), condition=%wide.region_6.9_spmd, body=%wide.region_3.8_spmd.sunk | while | flops 154624 | bytes 1353909 | solution.py:204
  190.9 1.5 scatter_custom_fusion.11
  192.7 1.5 scatter_custom_fusion.10
  195.0 25.8 %body.4 = f32[32,2,128]{2,1,0:T(2,128)} custom-call(f32[32,2,128]{2,1,0:T(2,128)} %reshape.1467.x_ref), custom_call_target="tpu_custom_call" | custom-call | tf_op jit(solution)/shard_map/while/body/eval_jaxpr/while/body/pallas_call | solution.py:134
  232.6 33.5 %while.53 = (s32[]{:T(128)}, f32[8,512]{1,0:T(8,128)S(1)}, s32[]{:T(128)}, s32[2,256]{1,0:T(2,128)S(1)}, f32[8,1,256]{2,1,0:T(1,128)S(1)}, /*index=5*/f32[8,1,25...) while((s32[]{:T(128)}, f32[8,512]{1,0:T(8,128)S(1)}, ...), condition=%wide.region_6.9_spmd, body=%wide.region_3.8_spmd.sunk | while | flops 154624 | bytes 1353909 | solution.py:204
  239.0 25.8 %body.4 = f32[32,2,128]{2,1,0:T(2,128)} custom-call(f32[32,2,128]{2,1,0:T(2,128)} %reshape.1467.x_ref), custom_call_target="tpu_custom_call" | custom-call | tf_op jit(solution)/shard_map/while/body/eval_jaxpr/while/body/pallas_call | solution.py:134
  (505 shorter events, 60.9 us)
Async XLA Ops:
  0.6 46.2 %copy-start.4 = (f32[8]{0:T(128)S(1)}, f32[8]{0:T(128)}, u32[]{:S(2)}) copy-start(f32[8]{0:T(128)} %constant.227.clone.1) | copy-start | bytes 100
  2.2 53.1 %all-to-all-start = ((bf16[2,8,16,256]{3,1,0,2:T(8,128)(2,1)}), bf16[2,8,16,256]{3,1,0,2:T(8,128)(2,1)S(1)}, u32[]{:S(2)}, u32[]{:S(2)}) async-start(bf16[2,8,16,256]{3,1,0,2:T(8,128)(2,1)} %copy.1121), calls=%async_computation | async-start | bytes 262144 | tf_op jit(solution)/shard_map/all_to_all | solution.py:169
  55.2 2.1 copy-start.3
  55.3 2.1 copy-start
  55.3 2.1 copy-start.2
  55.3 2.1 copy-start.5
  55.3 2.1 copy-start.6
  55.3 2.1 copy-start.7
  269.4 1.3 copy-start.1

commit v4 on v3

--- a/solution.py
+++ b/solution.py
@@ -77,7 +77,40 @@
     return matmul_two(numerator, inverse)
 
 
-def all_reduce_kernel(nb, nz, x_ref, o_ref, r1, r2, r3, s1, q1, s2, q2, s3, q3):
+def split_three(x):
+    hi = x.astype(jnp.bfloat16)
+    rest = x - hi.astype(jnp.float32)
+    mid = rest.astype(jnp.bfloat16)
+    lo = (rest - mid.astype(jnp.float32)).astype(jnp.bfloat16)
+    return (hi, mid, lo)
+
+
+def gather_cols(parts, onehot):
+    out = None
+    for part in parts:
+        term = jnp.dot(part, onehot, preferred_element_type=jnp.float32)
+        out = term if out is None else out + term
+    return out
+
+
+def scatter_cols(values, onehot):
+    out = None
+    for part in split_three(values):
+        term = lax.dot_general(
+            part, onehot, (((1,), (1,)), ((), ())), preferred_element_type=jnp.float32
+        )
+        out = term if out is None else out + term
+    return out
+
+
+def rows_of(x):
+    return [x[i : i + 1, :] for i in range(x.shape[0])]
+
+
+def round_kernel(
+    nb, nz, gain_ref, target_ref, coher_ref, onehot_p_ref, onehot_q_ref, damp_ref, o_ref,
+    pay, r1, r2, r3, s1, q1, s2, q2, s3, q3,
+):
     mz = lax.axis_index("dir")
     mb = lax.axis_index("bl")
     z_peers = [lax.rem(mz + k, nz) for k in range(1, nz)]
@@ -88,6 +121,37 @@
         pl.semaphore_signal(barrier, 1, device_id=(p, mz), device_id_type=MESH_ID)
     for p in z_peers:
         pl.semaphore_signal(barrier, 1, device_id=(mb, p), device_id_type=MESH_ID)
+
+    gain_now = gain_ref[...]
+    parts = split_three(gain_now)
+    gain_p = rows_of(gather_cols(parts, onehot_p_ref[...]))
+    gain_q = rows_of(gather_cols(parts, onehot_q_ref[...]))
+    coher_now = rows_of(coher_ref[...])
+    target = rows_of(target_ref[...])
+    z_rows = matmul_rows(coher_now, adjoint_rows(gain_q))
+    y_rows = matmul_rows(adjoint_rows(coher_now), adjoint_rows(gain_p))
+    zero_row = jnp.zeros_like(target[0])
+    leading = (
+        matmul_rows(target, adjoint_rows(z_rows))
+        + gram_rows(matmul_rows(z_rows, adjoint_rows(z_rows)))
+        + [zero_row] * 4
+    )
+    second = (
+        matmul_rows(adjoint_rows(target), adjoint_rows(y_rows))
+        + gram_rows(matmul_rows(y_rows, adjoint_rows(y_rows)))
+        + [zero_row] * 4
+    )
+    sums = scatter_cols(jnp.concatenate(leading, 0), onehot_p_ref[...]) + scatter_cols(
+        jnp.concatenate(second, 0), onehot_q_ref[...]
+    )
+    groups = sums.shape[1] // 128
+    pairs = sums.shape[0] // 2
+    per = pay.shape[1]
+    for g in range(groups):
+        for h in range(pairs):
+            slab = g * pairs + h
+            pay[slab // per, slab % per] = sums[2 * h : 2 * h + 2, 128 * g : 128 * g + 128]
+
     pl.semaphore_wait(barrier, (nz - 1) + (nb - 1))
 
     def exchange(peers, src_of, buf, me, send_sems, recv_sems, device_of):
@@ -115,8 +179,8 @@
         for c in sent:
             c.wait_send()
 
-    exchange(b_peers, lambda p: x_ref.at[p], r1, mb, s1, q1, lambda p: (p, mz))
-    own = x_ref[mb]
+    exchange(b_peers, lambda p: pay.at[p], r1, mb, s1, q1, lambda p: (p, mz))
+    own = pay[mb]
     for p in b_peers:
         own = own + r1[p]
     r2[mz] = own
@@ -126,20 +190,70 @@
         total = total + r2[p]
     r3[mb] = total
     exchange(b_peers, lambda p: r3.at[mb], r3, mb, s3, q3, lambda p: (p, mz))
-    o_ref[...] = r3[...]
-
-
-def all_reduce(payload, nb, nz):
-    chunk_shape = payload.shape[1:]
+
+    gathered = []
+    for h in range(pairs):
+        for t in range(2):
+            pieces = []
+            for g in range(groups):
+                slab = g * pairs + h
+                pieces.append(r3[slab // per, slab % per, t : t + 1, :])
+            gathered.append(jnp.concatenate(pieces, 1))
+    damp_value = damp_ref[0, 0]
+    gain_rows = rows_of(gain_now)
+    numerator = [gathered[i] + damp_value * gain_rows[i] for i in range(8)]
+    diag_a = gathered[8] + damp_value
+    diag_d = gathered[9] + damp_value
+    cross_r = gathered[10]
+    cross_i = gathered[11]
+    determinant = diag_a * diag_d - cross_r * cross_r - cross_i * cross_i
+    zeros_row = jnp.zeros_like(determinant)
+    inverse = [
+        v / determinant
+        for v in (diag_d, zeros_row, -cross_r, -cross_i, -cross_r, cross_i, diag_a, zeros_row)
+    ]
+    o_ref[...] = jnp.concatenate(matmul_rows(numerator, inverse), 0)
+
+
+def matmul_rows(left, right):
+    pieces = []
+    for i in (0, 1):
+        for j in (0, 1):
+            left_r0, left_i0 = left[4 * i], left[4 * i + 1]
+            left_r1, left_i1 = left[4 * i + 2], left[4 * i + 3]
+            right_r0, right_i0 = right[2 * j], right[2 * j + 1]
+            right_r1, right_i1 = right[4 + 2 * j], right[4 + 2 * j + 1]
+            pieces.append(
+                left_r0 * right_r0 - left_i0 * right_i0 + left_r1 * right_r1 - left_i1 * right_i1
+            )
+            pieces.append(
+                left_r0 * right_i0 + left_i0 * right_r0 + left_r1 * right_i1 + left_i1 * right_r1
+            )
+    return pieces
+
+
+def adjoint_rows(mat):
+    return [mat[0], -mat[1], mat[4], -mat[5], mat[2], -mat[3], mat[6], -mat[7]]
+
+
+def gram_rows(gram):
+    return [gram[0], gram[6], gram[2], gram[3]]
+
+
+def damped_round(gain_now, target, coher_now, onehot_p, onehot_q, damp_value, nb, nz):
+    stations = gain_now.shape[1]
+    per = (16 * stations) // (nb * 2 * 128)
+    vmem = pl.BlockSpec(memory_space=pltpu.VMEM)
     return pl.pallas_call(
-        functools.partial(all_reduce_kernel, nb, nz),
-        out_shape=jax.ShapeDtypeStruct(payload.shape, payload.dtype),
-        in_specs=[pl.BlockSpec(memory_space=pltpu.VMEM)],
-        out_specs=pl.BlockSpec(memory_space=pltpu.VMEM),
+        functools.partial(round_kernel, nb, nz),
+        out_shape=jax.ShapeDtypeStruct(gain_now.shape, gain_now.dtype),
+        in_specs=[vmem] * 5 + [pl.BlockSpec(memory_space=pltpu.SMEM)],
+        out_specs=vmem,
         scratch_shapes=[
-            pltpu.VMEM((nb,) + chunk_shape, payload.dtype),
-            pltpu.VMEM((nz,) + chunk_shape, payload.dtype),
-            pltpu.VMEM((nb,) + chunk_shape, payload.dtype),
+            pltpu.VMEM((nb, per, 2, 128), jnp.float32),
+            pltpu.VMEM((nb, per, 2, 128), jnp.float32),
+            pltpu.VMEM((nz, per, 2, 128), jnp.float32),
+            pltpu.VMEM((nb, per, 2, 128), jnp.float32),
             pltpu.SemaphoreType.DMA((nb,)),
             pltpu.SemaphoreType.DMA((nb,)),
             pltpu.SemaphoreType.DMA((nz,)),
@@ -148,14 +262,7 @@
             pltpu.SemaphoreType.DMA((nb,)),
         ],
         compiler_params=pltpu.CompilerParams(collective_id=0, has_side_effects=True),
-    )(payload)
-
-
-def station_sum(rows, nz, nb):
-    width = rows.shape[0] * 16
-    padded = jnp.pad(rows, ((0, 0), (0, 16 - rows.shape[1])))
-    summed = all_reduce(padded.reshape(nb, width // (nb * 128), 128), nb, nz)
-    return summed.reshape(rows.shape[0], 16)[:, : rows.shape[1]]
+    )(gain_now, target, coher_now, onehot_p, onehot_q, damp_value.reshape(1, 1))
 
 
 def on_device(visibilities, coherencies, gain_offsets, stations, solve_order, counts, damping):
@@ -175,6 +282,10 @@
     first_model = jnp.sum(apply_gains(gain_p, coher_f32, gain_q), axis=1)
     first_residual = visibilities - first_model
 
+    station_ids = lax.broadcasted_iota(jnp.int32, (station_count, stations.shape[1]), 0)
+    onehot_p = (station_ids == stations[0][None, :]).astype(jnp.bfloat16)
+    onehot_q = (station_ids == stations[1][None, :]).astype(jnp.bfloat16)
+
     def direction_model(gain_now, coher_now):
         gain_p = jnp.take(gain_now, stations[0], axis=1)[:, None, :]
         gain_q = jnp.take(gain_now, stations[1], axis=1)[:, None, :]
@@ -191,14 +302,10 @@
         target = residual + direction_model(gain_start, coher_now)
 
         def iterate(round_index, gain_now):
-            gain_p = jnp.take(gain_now, stations[0], axis=1)[:, None, :]
-            gain_q = jnp.take(gain_now, stations[1], axis=1)[:, None, :]
-            leading_endpoint, second = station_terms(gain_p, gain_q, coher_now, target)
-            local_rows = jax.ops.segment_sum(
-                leading_endpoint.T, stations[0], station_count
-            ) + jax.ops.segment_sum(second.T, stations[1], station_count)
-            gathered_sums = station_sum(local_rows, nz, groups).T
-            return solve_station(gathered_sums, gain_now, damp_value)
+            return damped_round(
+                gain_now, target[:, 0, :], coher_now[:, 0, :], onehot_p, onehot_q, damp_value,
+                groups, nz,
+            )
 
         rounds = jnp.clip(counts[which], 0, LM_ITERS)
         gain_final = lax.fori_loop(0, rounds, iterate, gain_start)

time: 272 us -> 234 us (0.86)
  other arithmetic: 27.5 us -> 9.95 us
  local copies, waits for them, and re-layouts: 52.6 us -> 36.5 us
  Pallas kernels: 132 us -> 129 us
    scatter-add x10 -> x0, other arithmetic: 14.9 us -> none  [the longest x5 7.47 us: iterate(): jax.ops.segment_sum(second.T, stations[1], station_count)]
    reshape x10 -> x0, local copies, waits for them, and re-layouts: 8.28 us -> none  [the longest x5 4.51 us: station_sum(): return summed.reshape(rows.shape[0], 16)[:, :rows.shape[1]]]
    gather x20 -> x0, local copies, waits for them, and re-layouts: 7.9 us -> none  [the longest x10 3.96 us: iterate(): gain_p = jnp.take(gain_now, stations[0], axis=1)[:, None, :]]
    pallas_call x5, Pallas kernels: 132 us -> 129 us  [damped_round(): pl.pallas_call(functools.partial(round_kernel, nb, nz), out_shape=jax.Sha...]
where the time goes in v4:
time: 234 us; the launch traced here: 233 us
  Pallas kernels  129 us (55%)
  local copies, waits for them, and re-layouts  36.5 us (16%)
  blocking collectives  27.2 us (12%)
  starting transfers between devices  15.7 us (7%)
  loops' own time  13.9 us (6%)
  other arithmetic  9.95 us (4%)
    pallas_call x5, Pallas kernels, damped_round(): pl.pallas_call(functools.partial(round_kernel, nb, nz), out_shape=jax.Sha...  129 us
    all_gather x1, blocking collectives, on_device(): lax.all_gather(gain_offsets, 'bl', axis=2, tiled=True)  27.2 us
    all_to_all x1, starting transfers between devices, on_device(): coher_all = lax.all_to_all(coherencies, 'dir', 2, 0, tiled=True)  15.7 us
    another operation x1, loops' own time, on_device(): lax.fori_loop(0, SOLVED, sweep, (start, first_residual))  13.8 us
    gather x16, local copies, waits for them, and re-layouts, direction_model(): gain_p = jnp.take(gain_now, stations[0], axis=1)[:, None, :]  6.34 us
    gather x16, local copies, waits for them, and re-layouts, direction_model(): gain_q = jnp.take(gain_now, stations[1], axis=1)[:, None, :]  6.32 us
  transfers between devices with their start and end apart: 1, of which 0 were waited for; matrix products, arithmetic and copies ran while one was open for 4% of the time, Pallas kernels for 0%

profile of v4, /device:TPU:1, one launch (start us, length us, event | category | flops | bytes accessed | tf_op | source)
XLA Modules:
  0.0 232.9 jit_solution(5815358091924566878)
XLA Ops:
  0.6 1.6 copy.285
  2.2 15.7 %all-to-all-start = ((bf16[2,8,16,256]{3,1,0,2:T(8,128)(2,1)}), bf16[2,8,16,256]{3,1,0,2:T(8,128)(2,1)S(1)}, u32[]{:S(2)}, u32[]{:S(2)}) async-start(bf16[2,8,16,256]{3,1,0,2:T(8,128)(2,1)} %copy.285), calls=%async_computation | async-start | bytes 262144 | tf_op jit(solution)/shard_map/all_to_all | solution.py:276
  18.0 0.8 fusion.13
  18.8 0.9 copy.283
  19.7 27.2 %all_gather.3 = f32[32,8,512]{0,1,2:T(8,128)S(1)} all-gather(f32[32,8,16]{0,1,2:T(8,128)S(1)} %copy.283), channel_id=1, replica_groups=mesh['bl'=32,'dir'=16] {'bl'}, dimensions={2}, use_global_device_ids=true | all-gather | bytes 540672 | tf_op jit(solution)/shard_map/all_gather | solution.py:270
  47.1 0.9 copy.296
  48.0 2.0 gather_fusion.5
  50.0 1.6 copy.287
  51.6 2.0 gather_fusion.4
  53.6 1.6 copy.284
  57.4 174.2 %while.43 = (s32[]{:T(128)}, f32[32,8,512]{2,1,0:T(8,128)S(1)}, f32[8,1,256]{2,1,0:T(1,128)S(1)}, s32[32]{0:T(128)S(1)}, s32[32]{0:T(128)S(1)}, /*index=5*/s32[2...) while((s32[]{:T(128)}, f32[32,8,512]{2,1,0:T(8,128)S(1)}, ...), condition=%wide.region_5.0_spmd.clone, body=%wide.region_1.7_spmd.clone.sunk | while | flops 614938 | bytes 1245162 | solution.py:315
  64.7 28.4 %while.44 = (s32[]{:T(128)}, f32[8,512]{1,0:T(8,128)S(1)}, s32[]{:T(128)}, f32[8,1,256]{2,0,1:T(8,128)S(1)}, f32[8,1,256]{2,0,1:T(8,128)S(1)}, /*index=5*/f32[]{...) while((s32[]{:T(128)}, f32[8,512]{1,0:T(8,128)S(1)}, s32[]{:T(128)}, ...), condition=%wide.region_4.6_spmd, body=%wide.region_3.5_spmd.sunk | while | flops 2 | bytes 32861 | solution.py:311
  65.3 27.8 %body.1 = f32[8,512]{1,0:T(8,128)S(1)} custom-call(f32[8,512]{1,0:T(8,128)} %copy.362.gain_ref, f32[8,256]{1,0:T(8,128)S(1)} %bitcast.546, f32[8,256]{1,0:T(8,128)S(1)} %bitcast.547, bf16[512,256]{1,0:T(8,128)(2,1)S(1)} %get-tuple-element.673.onehot_p_ref, bf16[512,256]{1,0:T(8,128)(2,1)S(1)} %get-tuple-element.674.onehot_q_ref, f32[1,1]{1,0:T(1,128)} %bitcast.543.damp_ref), custom_call_target="tpu_custom_call" | custom-call | tf_op jit(solution)/shard_map/while/body/eval_jaxpr/while/body/pallas_call | solution.py:247
  94.0 0.7 gather_fusion.3
  103.7 25.8 %while.44 = (s32[]{:T(128)}, f32[8,512]{1,0:T(8,128)S(1)}, s32[]{:T(128)}, f32[8,1,256]{2,0,1:T(8,128)S(1)}, f32[8,1,256]{2,0,1:T(8,128)S(1)}, /*index=5*/f32[]{...) while((s32[]{:T(128)}, f32[8,512]{1,0:T(8,128)S(1)}, s32[]{:T(128)}, ...), condition=%wide.region_4.6_spmd, body=%wide.region_3.5_spmd.sunk | while | flops 2 | bytes 32861 | solution.py:311
  104.3 25.1 %body.1 = f32[8,512]{1,0:T(8,128)S(1)} custom-call(f32[8,512]{1,0:T(8,128)} %copy.362.gain_ref, f32[8,256]{1,0:T(8,128)S(1)} %bitcast.546, f32[8,256]{1,0:T(8,128)S(1)} %bitcast.547, bf16[512,256]{1,0:T(8,128)(2,1)S(1)} %get-tuple-element.673.onehot_p_ref, bf16[512,256]{1,0:T(8,128)(2,1)S(1)} %get-tuple-element.674.onehot_q_ref, f32[1,1]{1,0:T(1,128)} %bitcast.543.damp_ref), custom_call_target="tpu_custom_call" | custom-call | tf_op jit(solution)/shard_map/while/body/eval_jaxpr/while/body/pallas_call | solution.py:247
  130.4 0.7 gather_fusion.3
  140.0 51.8 %while.44 = (s32[]{:T(128)}, f32[8,512]{1,0:T(8,128)S(1)}, s32[]{:T(128)}, f32[8,1,256]{2,0,1:T(8,128)S(1)}, f32[8,1,256]{2,0,1:T(8,128)S(1)}, /*index=5*/f32[]{...) while((s32[]{:T(128)}, f32[8,512]{1,0:T(8,128)S(1)}, s32[]{:T(128)}, ...), condition=%wide.region_4.6_spmd, body=%wide.region_3.5_spmd.sunk | while | flops 2 | bytes 32861 | solution.py:311
  140.7 25.3 %body.1 = f32[8,512]{1,0:T(8,128)S(1)} custom-call(f32[8,512]{1,0:T(8,128)} %copy.362.gain_ref, f32[8,256]{1,0:T(8,128)S(1)} %bitcast.546, f32[8,256]{1,0:T(8,128)S(1)} %bitcast.547, bf16[512,256]{1,0:T(8,128)(2,1)S(1)} %get-tuple-element.673.onehot_p_ref, bf16[512,256]{1,0:T(8,128)(2,1)S(1)} %get-tuple-element.674.onehot_q_ref, f32[1,1]{1,0:T(1,128)} %bitcast.543.damp_ref), custom_call_target="tpu_custom_call" | custom-call | tf_op jit(solution)/shard_map/while/body/eval_jaxpr/while/body/pallas_call | solution.py:247
  166.6 25.2 %body.1 = f32[8,512]{1,0:T(8,128)S(1)} custom-call(f32[8,512]{1,0:T(8,128)} %copy.362.gain_ref, f32[8,256]{1,0:T(8,128)S(1)} %bitcast.546, f32[8,256]{1,0:T(8,128)S(1)} %bitcast.547, bf16[512,256]{1,0:T(8,128)(2,1)S(1)} %get-tuple-element.673.onehot_p_ref, bf16[512,256]{1,0:T(8,128)(2,1)S(1)} %get-tuple-element.674.onehot_q_ref, f32[1,1]{1,0:T(1,128)} %bitcast.543.damp_ref), custom_call_target="tpu_custom_call" | custom-call | tf_op jit(solution)/shard_map/while/body/eval_jaxpr/while/body/pallas_call | solution.py:247
  192.7 0.7 gather_fusion.3
  202.4 25.9 %while.44 = (s32[]{:T(128)}, f32[8,512]{1,0:T(8,128)S(1)}, s32[]{:T(128)}, f32[8,1,256]{2,0,1:T(8,128)S(1)}, f32[8,1,256]{2,0,1:T(8,128)S(1)}, /*index=5*/f32[]{...) while((s32[]{:T(128)}, f32[8,512]{1,0:T(8,128)S(1)}, s32[]{:T(128)}, ...), condition=%wide.region_4.6_spmd, body=%wide.region_3.5_spmd.sunk | while | flops 2 | bytes 32861 | solution.py:311
  203.0 25.2 %body.1 = f32[8,512]{1,0:T(8,128)S(1)} custom-call(f32[8,512]{1,0:T(8,128)} %copy.362.gain_ref, f32[8,256]{1,0:T(8,128)S(1)} %bitcast.546, f32[8,256]{1,0:T(8,128)S(1)} %bitcast.547, bf16[512,256]{1,0:T(8,128)(2,1)S(1)} %get-tuple-element.673.onehot_p_ref, bf16[512,256]{1,0:T(8,128)(2,1)S(1)} %get-tuple-element.674.onehot_q_ref, f32[1,1]{1,0:T(1,128)} %bitcast.543.damp_ref), custom_call_target="tpu_custom_call" | custom-call | tf_op jit(solution)/shard_map/while/body/eval_jaxpr/while/body/pallas_call | solution.py:247
  229.2 0.7 gather_fusion.3
  (231 shorter events, 32.2 us)
Async XLA Ops:
  0.6 46.2 %copy-start.4 = (f32[8]{0:T(128)S(1)}, f32[8]{0:T(128)}, u32[]{:S(2)}) copy-start(f32[8]{0:T(128)} %constant.171.clone.1) | copy-start | bytes 100
  2.2 53.1 %all-to-all-start = ((bf16[2,8,16,256]{3,1,0,2:T(8,128)(2,1)}), bf16[2,8,16,256]{3,1,0,2:T(8,128)(2,1)S(1)}, u32[]{:S(2)}, u32[]{:S(2)}) async-start(bf16[2,8,16,256]{3,1,0,2:T(8,128)(2,1)} %copy.285), calls=%async_computation | async-start | bytes 262144 | tf_op jit(solution)/shard_map/all_to_all | solution.py:276
  55.2 2.1 copy-start.3
  55.2 2.1 copy-start.1
  55.2 2.1 copy-start.2
  55.2 2.1 copy-start.5
  55.2 2.1 copy-start.6
  55.3 2.1 copy-start.7
  231.6 1.3 copy-start

commit v5 on v4

--- a/solution.py
+++ b/solution.py
@@ -267,8 +267,13 @@
 
 def on_device(visibilities, coherencies, gain_offsets, stations, solve_order, counts, damping):
     identity = jnp.zeros((8,), jnp.float32).at[0].set(1.0).at[6].set(1.0)
-    start = lax.all_gather(gain_offsets, "bl", axis=2, tiled=True) + identity[None, :, None]
     groups = lax.axis_size("bl")
+    copies = jnp.broadcast_to(gain_offsets[None], (groups,) + gain_offsets.shape)
+    blocks = lax.all_to_all(copies, "bl", 0, 0, tiled=True)
+    offsets = jnp.transpose(blocks, (1, 2, 0, 3)).reshape(
+        gain_offsets.shape[:2] + (groups * gain_offsets.shape[2],)
+    )
+    start = offsets + identity[None, :, None]
     nz = lax.axis_size("dir")
     total_channels = coherencies.shape[2]
     station_count = start.shape[2]

time: 234 us -> 293 us (1.25)
  Pallas kernels: 129 us -> 175 us
  blocking collectives: 27.2 us -> 0 us
  waiting for transfers between devices: 0.01 us -> 20.7 us
  starting transfers between devices: 15.7 us -> 26.5 us
  local copies, waits for them, and re-layouts: 36.5 us -> 40.8 us
    pallas_call x5 -> x7, Pallas kernels: 129 us -> 175 us  [damped_round(): pl.pallas_call(functools.partial(round_kernel, nb, nz), out_shape=jax.Sha...]
    all_gather x1 -> x0, blocking collectives: 27.2 us -> none  [on_device(): lax.all_gather(gain_offsets, 'bl', axis=2, tiled=True)]
    all_to_all x0 -> x1, waiting for transfers between devices: none -> 11.5 us  [on_device(): blocks = lax.all_to_all(copies, 'bl', 0, 0, tiled=True)]
    all_to_all x0 -> x1, starting transfers between devices: none -> 10.7 us  [on_device(): blocks = lax.all_to_all(copies, 'bl', 0, 0, tiled=True)]
    all_to_all x1, waiting for transfers between devices: 0.01 us -> 9.25 us  [on_device(): coher_all = lax.all_to_all(coherencies, 'dir', 2, 0, tiled=True)]
  transfers between devices with their start and end apart: 1 -> 2, of which waited for: 0 -> 2; matrix products, arithmetic and copies ran while one was open for 4% -> 1% of each run, Pallas kernels for 0% -> 0%
where the time goes in v5:
time: 293 us; the launch traced here: 291 us
  Pallas kernels  175 us (60%)
  local copies, waits for them, and re-layouts  40.8 us (14%)
  starting transfers between devices  26.5 us (9%)
  waiting for transfers between devices  20.7 us (7%)
  loops' own time  14 us (5%)
  other arithmetic  12.8 us (4%)
    pallas_call x7, Pallas kernels, damped_round(): pl.pallas_call(functools.partial(round_kernel, nb, nz), out_shape=jax.Sha...  175 us
    all_to_all x1, starting transfers between devices, on_device(): coher_all = lax.all_to_all(coherencies, 'dir', 2, 0, tiled=True)  15.7 us
    another operation x1, loops' own time, on_device(): lax.fori_loop(0, SOLVED, sweep, (start, first_residual))  13.8 us
    all_to_all x1, waiting for transfers between devices, on_device(): blocks = lax.all_to_all(copies, 'bl', 0, 0, tiled=True)  11.5 us
    all_to_all x1, starting transfers between devices, on_device(): blocks = lax.all_to_all(copies, 'bl', 0, 0, tiled=True)  10.7 us
    all_to_all x1, waiting for transfers between devices, on_device(): coher_all = lax.all_to_all(coherencies, 'dir', 2, 0, tiled=True)  9.25 us
    gather x16, local copies, waits for them, and re-layouts, direction_model(): gain_p = jnp.take(gain_now, stations[0], axis=1)[:, None, :]  6.35 us
    gather x16, local copies, waits for them, and re-layouts, direction_model(): gain_q = jnp.take(gain_now, stations[1], axis=1)[:, None, :]  6.32 us
  transfers between devices with their start and end apart: 2, of which 2 were waited for; matrix products, arithmetic and copies ran while one was open for 1% of the time, Pallas kernels for 0%

profile of v5, /device:TPU:1, one launch (start us, length us, event | category | flops | bytes accessed | tf_op | source)
XLA Modules:
  0.0 291.1 jit_solution(7302107079075253044)
XLA Ops:
  0.6 1.6 copy.287
  2.3 15.7 %all-to-all-start.1 = ((bf16[2,8,16,256]{3,1,0,2:T(8,128)(2,1)}), bf16[2,8,16,256]{3,1,0,2:T(8,128)(2,1)S(1)}, u32[]{:S(2)}, u32[]{:S(2)}) async-start(bf16[2,8,16,256]{3,1,0,2:T(8,128)(2,1)} %copy.287), calls=%async_computation.1 | async-start | bytes 262144 | tf_op jit(solution)/shard_map/all_to_all | solution.py:281
  19.0 1.7 reshape.1035
  20.8 9.3 %all-to-all-done.1 = bf16[2,8,16,256]{3,1,0,2:T(8,128)(2,1)S(1)} async-done(((bf16[2,8,16,256]{3,1,0,2:T(8,128)(2,1)}), bf16[2,8,16,256]{3,1,0,2:T(8,128)(2,1)S(1)}, u32[]{:S(2)}, u32[]{:S(2)}) %all-to-all-start.1) | async-done | bytes 131104 | tf_op jit(solution)/shard_map/all_to_all | solution.py:281
  30.0 10.7 %all-to-all-start = ((f32[32,1,4096]{2,1,0:T(1,128)}), f32[32,1,4096]{2,1,0:T(1,128)S(1)}, u32[]{:S(2)}, u32[]{:S(2)}) async-start(f32[32,1,4096]{2,1,0:T(1,128)} %reshape.1035), calls=%async_computation | async-start | bytes 1048576 | tf_op jit(solution)/shard_map/all_to_all | solution.py:272
  40.8 11.5 %all-to-all-done = f32[32,1,4096]{2,1,0:T(1,128)S(1)} async-done(((f32[32,1,4096]{2,1,0:T(1,128)}), f32[32,1,4096]{2,1,0:T(1,128)S(1)}, u32[]{:S(2)}, u32[]{:S(2)}) %all-to-all-start) | async-done | bytes 524320 | tf_op jit(solution)/shard_map/all_to_all | solution.py:272
  52.8 1.9 reduce.17
  56.2 1.2 copy_add_fusion
  57.4 2.0 gather_fusion.5
  59.5 1.6 copy.289
  61.0 2.0 gather_fusion.4
  63.0 1.6 copy.286
  67.7 222.0 %while.43 = (s32[]{:T(128)}, f32[32,8,512]{2,1,0:T(8,128)S(1)}, f32[8,1,256]{2,1,0:T(1,128)S(1)}, s32[32]{0:T(128)S(1)}, s32[32]{0:T(128)S(1)}, /*index=5*/s32[2...) while((s32[]{:T(128)}, f32[32,8,512]{2,1,0:T(8,128)S(1)}, ...), condition=%wide.region_5.0_spmd.clone, body=%wide.region_1.7_spmd.clone.sunk | while | flops 614938 | bytes 1245162 | solution.py:320
  75.0 51.3 %while.44 = (s32[]{:T(128)}, f32[8,512]{1,0:T(8,128)S(1)}, s32[]{:T(128)}, f32[8,1,256]{2,0,1:T(8,128)S(1)}, f32[8,1,256]{2,0,1:T(8,128)S(1)}, /*index=5*/f32[]{...) while((s32[]{:T(128)}, f32[8,512]{1,0:T(8,128)S(1)}, s32[]{:T(128)}, ...), condition=%wide.region_4.6_spmd, body=%wide.region_3.5_spmd.sunk | while | flops 2 | bytes 32861 | solution.py:316
  75.6 25.1 %body.1 = f32[8,512]{1,0:T(8,128)S(1)} custom-call(f32[8,512]{1,0:T(8,128)} %copy.365.gain_ref, f32[8,256]{1,0:T(8,128)S(1)} %bitcast.554, f32[8,256]{1,0:T(8,128)S(1)} %bitcast.555, bf16[512,256]{1,0:T(8,128)(2,1)S(1)} %get-tuple-element.673.onehot_p_ref, bf16[512,256]{1,0:T(8,128)(2,1)S(1)} %get-tuple-element.674.onehot_q_ref, f32[1,1]{1,0:T(1,128)} %bitcast.550.damp_ref), custom_call_target="tpu_custom_call" | custom-call | tf_op jit(solution)/shard_map/while/body/eval_jaxpr/while/body/pallas_call | solution.py:247
  101.3 25.0 %body.1 = f32[8,512]{1,0:T(8,128)S(1)} custom-call(f32[8,512]{1,0:T(8,128)} %copy.365.gain_ref, f32[8,256]{1,0:T(8,128)S(1)} %bitcast.554, f32[8,256]{1,0:T(8,128)S(1)} %bitcast.555, bf16[512,256]{1,0:T(8,128)(2,1)S(1)} %get-tuple-element.673.onehot_p_ref, bf16[512,256]{1,0:T(8,128)(2,1)S(1)} %get-tuple-element.674.onehot_q_ref, f32[1,1]{1,0:T(1,128)} %bitcast.550.damp_ref), custom_call_target="tpu_custom_call" | custom-call | tf_op jit(solution)/shard_map/while/body/eval_jaxpr/while/body/pallas_call | solution.py:247
  136.9 25.6 %while.44 = (s32[]{:T(128)}, f32[8,512]{1,0:T(8,128)S(1)}, s32[]{:T(128)}, f32[8,1,256]{2,0,1:T(8,128)S(1)}, f32[8,1,256]{2,0,1:T(8,128)S(1)}, /*index=5*/f32[]{...) while((s32[]{:T(128)}, f32[8,512]{1,0:T(8,128)S(1)}, s32[]{:T(128)}, ...), condition=%wide.region_4.6_spmd, body=%wide.region_3.5_spmd.sunk | while | flops 2 | bytes 32861 | solution.py:316
  137.5 25.0 %body.1 = f32[8,512]{1,0:T(8,128)S(1)} custom-call(f32[8,512]{1,0:T(8,128)} %copy.365.gain_ref, f32[8,256]{1,0:T(8,128)S(1)} %bitcast.554, f32[8,256]{1,0:T(8,128)S(1)} %bitcast.555, bf16[512,256]{1,0:T(8,128)(2,1)S(1)} %get-tuple-element.673.onehot_p_ref, bf16[512,256]{1,0:T(8,128)(2,1)S(1)} %get-tuple-element.674.onehot_q_ref, f32[1,1]{1,0:T(1,128)} %bitcast.550.damp_ref), custom_call_target="tpu_custom_call" | custom-call | tf_op jit(solution)/shard_map/while/body/eval_jaxpr/while/body/pallas_call | solution.py:247
  173.0 51.2 %while.44 = (s32[]{:T(128)}, f32[8,512]{1,0:T(8,128)S(1)}, s32[]{:T(128)}, f32[8,1,256]{2,0,1:T(8,128)S(1)}, f32[8,1,256]{2,0,1:T(8,128)S(1)}, /*index=5*/f32[]{...) while((s32[]{:T(128)}, f32[8,512]{1,0:T(8,128)S(1)}, s32[]{:T(128)}, ...), condition=%wide.region_4.6_spmd, body=%wide.region_3.5_spmd.sunk | while | flops 2 | bytes 32861 | solution.py:316
  173.7 25.0 %body.1 = f32[8,512]{1,0:T(8,128)S(1)} custom-call(f32[8,512]{1,0:T(8,128)} %copy.365.gain_ref, f32[8,256]{1,0:T(8,128)S(1)} %bitcast.554, f32[8,256]{1,0:T(8,128)S(1)} %bitcast.555, bf16[512,256]{1,0:T(8,128)(2,1)S(1)} %get-tuple-element.673.onehot_p_ref, bf16[512,256]{1,0:T(8,128)(2,1)S(1)} %get-tuple-element.674.onehot_q_ref, f32[1,1]{1,0:T(1,128)} %bitcast.550.damp_ref), custom_call_target="tpu_custom_call" | custom-call | tf_op jit(solution)/shard_map/while/body/eval_jaxpr/while/body/pallas_call | solution.py:247
  199.3 25.0 %body.1 = f32[8,512]{1,0:T(8,128)S(1)} custom-call(f32[8,512]{1,0:T(8,128)} %copy.365.gain_ref, f32[8,256]{1,0:T(8,128)S(1)} %bitcast.554, f32[8,256]{1,0:T(8,128)S(1)} %bitcast.555, bf16[512,256]{1,0:T(8,128)(2,1)S(1)} %get-tuple-element.673.onehot_p_ref, bf16[512,256]{1,0:T(8,128)(2,1)S(1)} %get-tuple-element.674.onehot_q_ref, f32[1,1]{1,0:T(1,128)} %bitcast.550.damp_ref), custom_call_target="tpu_custom_call" | custom-call | tf_op jit(solution)/shard_map/while/body/eval_jaxpr/while/body/pallas_call | solution.py:247
  234.8 51.6 %while.44 = (s32[]{:T(128)}, f32[8,512]{1,0:T(8,128)S(1)}, s32[]{:T(128)}, f32[8,1,256]{2,0,1:T(8,128)S(1)}, f32[8,1,256]{2,0,1:T(8,128)S(1)}, /*index=5*/f32[]{...) while((s32[]{:T(128)}, f32[8,512]{1,0:T(8,128)S(1)}, s32[]{:T(128)}, ...), condition=%wide.region_4.6_spmd, body=%wide.region_3.5_spmd.sunk | while | flops 2 | bytes 32861 | solution.py:316
  235.4 25.1 %body.1 = f32[8,512]{1,0:T(8,128)S(1)} custom-call(f32[8,512]{1,0:T(8,128)} %copy.365.gain_ref, f32[8,256]{1,0:T(8,128)S(1)} %bitcast.554, f32[8,256]{1,0:T(8,128)S(1)} %bitcast.555, bf16[512,256]{1,0:T(8,128)(2,1)S(1)} %get-tuple-element.673.onehot_p_ref, bf16[512,256]{1,0:T(8,128)(2,1)S(1)} %get-tuple-element.674.onehot_q_ref, f32[1,1]{1,0:T(1,128)} %bitcast.550.damp_ref), custom_call_target="tpu_custom_call" | custom-call | tf_op jit(solution)/shard_map/while/body/eval_jaxpr/while/body/pallas_call | solution.py:247
  261.2 25.2 %body.1 = f32[8,512]{1,0:T(8,128)S(1)} custom-call(f32[8,512]{1,0:T(8,128)} %copy.365.gain_ref, f32[8,256]{1,0:T(8,128)S(1)} %bitcast.554, f32[8,256]{1,0:T(8,128)S(1)} %bitcast.555, bf16[512,256]{1,0:T(8,128)(2,1)S(1)} %get-tuple-element.673.onehot_p_ref, bf16[512,256]{1,0:T(8,128)(2,1)S(1)} %get-tuple-element.674.onehot_q_ref, f32[1,1]{1,0:T(1,128)} %bitcast.550.damp_ref), custom_call_target="tpu_custom_call" | custom-call | tf_op jit(solution)/shard_map/while/body/eval_jaxpr/while/body/pallas_call | solution.py:247
  (244 shorter events, 40.0 us)
Async XLA Ops:
  0.6 18.2 %copy-start = (f32[32,8,16]{0,2,1:T(8,128)S(1)}, f32[32,8,16]{0,2,1:T(8,128)}, u32[]{:S(2)}) copy-start(f32[32,8,16]{0,2,1:T(8,128)} %param.23) | copy-start | bytes 49156
  2.3 27.8 %all-to-all-start.1 = ((bf16[2,8,16,256]{3,1,0,2:T(8,128)(2,1)}), bf16[2,8,16,256]{3,1,0,2:T(8,128)(2,1)S(1)}, u32[]{:S(2)}, u32[]{:S(2)}) async-start(bf16[2,8,16,256]{3,1,0,2:T(8,128)(2,1)} %copy.287), calls=%async_computation.1 | async-start | bytes 262144 | tf_op jit(solution)/shard_map/all_to_all | solution.py:281
  30.0 22.3 %all-to-all-start = ((f32[32,1,4096]{2,1,0:T(1,128)}), f32[32,1,4096]{2,1,0:T(1,128)S(1)}, u32[]{:S(2)}, u32[]{:S(2)}) async-start(f32[32,1,4096]{2,1,0:T(1,128)} %reshape.1035), calls=%async_computation | async-start | bytes 1048576 | tf_op jit(solution)/shard_map/all_to_all | solution.py:272
  55.6 0.7 copy-start.5
  65.8 1.8 copy-start.4
  65.8 1.8 copy-start.2
  65.8 1.8 copy-start.3
  65.8 1.8 copy-start.6
  65.9 1.8 copy-start.7
  65.9 1.8 copy-start.8
  289.8 1.3 copy-start.1

commit v6 on v4

--- a/solution.py
+++ b/solution.py
@@ -265,15 +265,110 @@
     )(gain_now, target, coher_now, onehot_p, onehot_q, damp_value.reshape(1, 1))
 
 
+def prologue_kernel(nb, nz, coh_ref, gain_ref, coh_out, gain_out, coh_buf, gain_buf, s1, q1, s2, q2):
+    mz = lax.axis_index("dir")
+    mb = lax.axis_index("bl")
+    z_peers = [lax.rem(mz + k, nz) for k in range(1, nz)]
+    b_peers = [lax.rem(mb + k, nb) for k in range(1, nb)]
+
+    barrier = pltpu.get_barrier_semaphore()
+    for p in b_peers:
+        pl.semaphore_signal(barrier, 1, device_id=(p, mz), device_id_type=MESH_ID)
+    for p in z_peers:
+        pl.semaphore_signal(barrier, 1, device_id=(mb, p), device_id_type=MESH_ID)
+    pl.semaphore_wait(barrier, (nz - 1) + (nb - 1))
+
+    sent = []
+    for p in z_peers:
+        c = pltpu.make_async_remote_copy(
+            src_ref=coh_ref.at[p],
+            dst_ref=coh_buf.at[mz],
+            send_sem=s1.at[p],
+            recv_sem=q1.at[mz],
+            device_id=(mb, p),
+            device_id_type=MESH_ID,
+        )
+        c.start()
+        sent.append(c)
+    for p in b_peers:
+        c = pltpu.make_async_remote_copy(
+            src_ref=gain_ref,
+            dst_ref=gain_buf.at[mb],
+            send_sem=s2.at[p],
+            recv_sem=q2.at[mb],
+            device_id=(p, mz),
+            device_id_type=MESH_ID,
+        )
+        c.start()
+        sent.append(c)
+    coh_buf[mz] = coh_ref[mz]
+    gain_buf[mb] = gain_ref[...]
+    for p in z_peers:
+        pltpu.make_async_remote_copy(
+            src_ref=coh_buf.at[p],
+            dst_ref=coh_buf.at[p],
+            send_sem=s1.at[p],
+            recv_sem=q1.at[p],
+            device_id=(mb, p),
+            device_id_type=MESH_ID,
+        ).wait_recv()
+    for p in b_peers:
+        pltpu.make_async_remote_copy(
+            src_ref=gain_buf.at[p],
+            dst_ref=gain_buf.at[p],
+            send_sem=s2.at[p],
+            recv_sem=q2.at[p],
+            device_id=(p, mz),
+            device_id_type=MESH_ID,
+        ).wait_recv()
+    for c in sent:
+        c.wait_send()
+    coh_out[...] = coh_buf[...]
+    gain_out[...] = gain_buf[...]
+
+
+def exchange_inputs(coh_by_channel, gain_block, nb, nz):
+    vmem = pl.BlockSpec(memory_space=pltpu.VMEM)
+    coh_shape = (nz,) + coh_by_channel.shape[1:]
+    gain_shape = (nb,) + gain_block.shape
+    return pl.pallas_call(
+        functools.partial(prologue_kernel, nb, nz),
+        out_shape=(
+            jax.ShapeDtypeStruct(coh_shape, coh_by_channel.dtype),
+            jax.ShapeDtypeStruct(gain_shape, gain_block.dtype),
+        ),
+        in_specs=[vmem, vmem],
+        out_specs=(vmem, vmem),
+        scratch_shapes=[
+            pltpu.VMEM(coh_shape, coh_by_channel.dtype),
+            pltpu.VMEM(gain_shape, gain_block.dtype),
+            pltpu.SemaphoreType.DMA((nz,)),
+            pltpu.SemaphoreType.DMA((nz,)),
+            pltpu.SemaphoreType.DMA((nb,)),
+            pltpu.SemaphoreType.DMA((nb,)),
+        ],
+        compiler_params=pltpu.CompilerParams(collective_id=1, has_side_effects=True),
+    )(coh_by_channel, gain_block)
+
+
 def on_device(visibilities, coherencies, gain_offsets, stations, solve_order, counts, damping):
     identity = jnp.zeros((8,), jnp.float32).at[0].set(1.0).at[6].set(1.0)
-    start = lax.all_gather(gain_offsets, "bl", axis=2, tiled=True) + identity[None, :, None]
     groups = lax.axis_size("bl")
     nz = lax.axis_size("dir")
+    owned, _, channels_all, width = coherencies.shape
+    by_channel = jnp.transpose(coherencies, (2, 0, 1, 3)).reshape(channels_all, owned * 8, width)
+    coh_recv, gain_recv = exchange_inputs(
+        by_channel, gain_offsets.reshape(-1, 128), groups, nz
+    )
+    direction_total = gain_offsets.shape[0]
+    offsets = jnp.transpose(
+        gain_recv.reshape((groups,) + gain_offsets.shape), (1, 2, 0, 3)
+    ).reshape(direction_total, 8, groups * gain_offsets.shape[2])
+    start = offsets + identity[None, :, None]
+    coher_all = coh_recv.reshape(nz * owned, 8, 1, width)
     total_channels = coherencies.shape[2]
     station_count = start.shape[2]
     damping_factor = visibilities.shape[2] * groups * total_channels / station_count
-    coher_all = lax.all_to_all(coherencies, "dir", 2, 0, tiled=True)
     ends_p = jnp.take(start, stations[0], axis=2)
     ends_q = jnp.take(start, stations[1], axis=2)
     gain_p = jnp.transpose(ends_p, (1, 0, 2))[:, :, None, :]

time: 234 us -> 274 us (1.17)
  Pallas kernels: 129 us -> 206 us
  blocking collectives: 27.2 us -> 0 us
  starting transfers between devices: 15.7 us -> 0 us
  local copies, waits for them, and re-layouts: 36.5 us -> 39.9 us
    pallas_call x5 -> x7, Pallas kernels: 129 us -> 176 us  [damped_round(): pl.pallas_call(functools.partial(round_kernel, nb, nz), out_shape=jax.Sha...]
    pallas_call x0 -> x1, Pallas kernels: none -> 30.2 us  [exchange_inputs(): pl.pallas_call(functools.partial(prologue_kernel, nb, nz), out_shape=(jax...]
    all_gather x1 -> x0, blocking collectives: 27.2 us -> none  [on_device(): lax.all_gather(gain_offsets, 'bl', axis=2, tiled=True)]
    all_to_all x1 -> x0, starting transfers between devices: 15.7 us -> none  [on_device(): coher_all = lax.all_to_all(coherencies, 'dir', 2, 0, tiled=True)]
  transfers between devices with their start and end apart: 1 -> 0, of which waited for: 0 -> 0; matrix products, arithmetic and copies ran while one was open for 4% -> 0% of each run, Pallas kernels for 0% -> 0%
where the time goes in v6:
time: 274 us; the launch traced here: 272 us
  Pallas kernels  206 us (75%)
  local copies, waits for them, and re-layouts  39.9 us (15%)
  loops' own time  14 us (5%)
  other arithmetic  11 us (4%)
    pallas_call x7, Pallas kernels, damped_round(): pl.pallas_call(functools.partial(round_kernel, nb, nz), out_shape=jax.Sha...  176 us
    pallas_call x1, Pallas kernels, exchange_inputs(): pl.pallas_call(functools.partial(prologue_kernel, nb, nz), out_shape=(jax...  30.2 us
    another operation x1, loops' own time, on_device(): lax.fori_loop(0, SOLVED, sweep, (start, first_residual))  13.8 us
    gather x16, local copies, waits for them, and re-layouts, direction_model(): gain_p = jnp.take(gain_now, stations[0], axis=1)[:, None, :]  6.35 us
    gather x16, local copies, waits for them, and re-layouts, direction_model(): gain_q = jnp.take(gain_now, stations[1], axis=1)[:, None, :]  6.32 us

profile of v6, /device:TPU:1, one launch (start us, length us, event | category | flops | bytes accessed | tf_op | source)
XLA Modules:
  0.0 272.3 jit_solution(12363392518364774901)
XLA Ops:
  0.6 1.6 copy.240
  2.2 1.5 copy.211.gain_ref
  3.7 30.2 %shard_map.86 = (bf16[16,16,256]{2,1,0:T(8,128)(2,1)S(1)}, f32[32,32,128]{2,1,0:T(8,128)}) custom-call(bf16[16,16,256]{2,1,0:T(8,128)(2,1)} %bitcast.554, f32[32,128]{1,0:T(8,128)} %copy.211.gain_ref), custom_call_target="tpu_custom_call" | custom-call | tf_op jit(solution)/shard_map/pallas_call | solution.py:334
  33.9 1.6 copy.212
  36.2 1.2 copy_add_fusion
  37.5 0.9 copy.226
  38.4 2.0 gather_fusion.5
  40.5 1.6 copy.217
  42.1 2.0 gather_fusion.4
  44.1 1.6 copy.215
  47.8 223.2 %while.43 = (s32[]{:T(128)}, f32[32,8,512]{2,1,0:T(8,128)S(1)}, f32[8,1,256]{2,1,0:T(1,128)S(1)}, s32[32]{0:T(128)S(1)}, s32[32]{0:T(128)S(1)}, /*index=5*/s32[2...) while((s32[]{:T(128)}, f32[32,8,512]{2,1,0:T(8,128)S(1)}, ...), condition=%wide.region_5.0_spmd.clone, body=%wide.region_1.7_spmd.clone.sunk | while | flops 614938 | bytes 1245170 | solution.py:410
  55.1 25.7 %while.44 = (s32[]{:T(128)}, f32[8,512]{1,0:T(8,128)S(1)}, s32[]{:T(128)}, f32[8,1,256]{2,0,1:T(8,128)S(1)}, f32[8,1,256]{2,0,1:T(8,128)S(1)}, /*index=5*/f32[]{...) while((s32[]{:T(128)}, f32[8,512]{1,0:T(8,128)S(1)}, s32[]{:T(128)}, ...), condition=%wide.region_4.6_spmd, body=%wide.region_3.5_spmd.sunk | while | flops 2 | bytes 32861 | solution.py:406
  55.7 25.0 %body.1 = f32[8,512]{1,0:T(8,128)S(1)} custom-call(f32[8,512]{1,0:T(8,128)} %copy.295.gain_ref, f32[8,256]{1,0:T(8,128)S(1)} %bitcast.552, f32[8,256]{1,0:T(8,128)S(1)} %bitcast.553, bf16[512,256]{1,0:T(8,128)(2,1)S(1)} %get-tuple-element.669.onehot_p_ref, bf16[512,256]{1,0:T(8,128)(2,1)S(1)} %get-tuple-element.670.onehot_q_ref, f32[1,1]{1,0:T(1,128)} %bitcast.547.damp_ref), custom_call_target="tpu_custom_call" | custom-call | tf_op jit(solution)/shard_map/while/body/eval_jaxpr/while/body/pallas_call | solution.py:247
  83.1 0.7 gather_fusion.3
  91.4 51.6 %while.44 = (s32[]{:T(128)}, f32[8,512]{1,0:T(8,128)S(1)}, s32[]{:T(128)}, f32[8,1,256]{2,0,1:T(8,128)S(1)}, f32[8,1,256]{2,0,1:T(8,128)S(1)}, /*index=5*/f32[]{...) while((s32[]{:T(128)}, f32[8,512]{1,0:T(8,128)S(1)}, s32[]{:T(128)}, ...), condition=%wide.region_4.6_spmd, body=%wide.region_3.5_spmd.sunk | while | flops 2 | bytes 32861 | solution.py:406
  92.0 25.1 %body.1 = f32[8,512]{1,0:T(8,128)S(1)} custom-call(f32[8,512]{1,0:T(8,128)} %copy.295.gain_ref, f32[8,256]{1,0:T(8,128)S(1)} %bitcast.552, f32[8,256]{1,0:T(8,128)S(1)} %bitcast.553, bf16[512,256]{1,0:T(8,128)(2,1)S(1)} %get-tuple-element.669.onehot_p_ref, bf16[512,256]{1,0:T(8,128)(2,1)S(1)} %get-tuple-element.670.onehot_q_ref, f32[1,1]{1,0:T(1,128)} %bitcast.547.damp_ref), custom_call_target="tpu_custom_call" | custom-call | tf_op jit(solution)/shard_map/while/body/eval_jaxpr/while/body/pallas_call | solution.py:247
  117.7 25.2 %body.1 = f32[8,512]{1,0:T(8,128)S(1)} custom-call(f32[8,512]{1,0:T(8,128)} %copy.295.gain_ref, f32[8,256]{1,0:T(8,128)S(1)} %bitcast.552, f32[8,256]{1,0:T(8,128)S(1)} %bitcast.553, bf16[512,256]{1,0:T(8,128)(2,1)S(1)} %get-tuple-element.669.onehot_p_ref, bf16[512,256]{1,0:T(8,128)(2,1)S(1)} %get-tuple-element.670.onehot_q_ref, f32[1,1]{1,0:T(1,128)} %bitcast.547.damp_ref), custom_call_target="tpu_custom_call" | custom-call | tf_op jit(solution)/shard_map/while/body/eval_jaxpr/while/body/pallas_call | solution.py:247
  145.2 0.7 gather_fusion.3
  153.5 51.8 %while.44 = (s32[]{:T(128)}, f32[8,512]{1,0:T(8,128)S(1)}, s32[]{:T(128)}, f32[8,1,256]{2,0,1:T(8,128)S(1)}, f32[8,1,256]{2,0,1:T(8,128)S(1)}, /*index=5*/f32[]{...) while((s32[]{:T(128)}, f32[8,512]{1,0:T(8,128)S(1)}, s32[]{:T(128)}, ...), condition=%wide.region_4.6_spmd, body=%wide.region_3.5_spmd.sunk | while | flops 2 | bytes 32861 | solution.py:406
  154.2 25.3 %body.1 = f32[8,512]{1,0:T(8,128)S(1)} custom-call(f32[8,512]{1,0:T(8,128)} %copy.295.gain_ref, f32[8,256]{1,0:T(8,128)S(1)} %bitcast.552, f32[8,256]{1,0:T(8,128)S(1)} %bitcast.553, bf16[512,256]{1,0:T(8,128)(2,1)S(1)} %get-tuple-element.669.onehot_p_ref, bf16[512,256]{1,0:T(8,128)(2,1)S(1)} %get-tuple-element.670.onehot_q_ref, f32[1,1]{1,0:T(1,128)} %bitcast.547.damp_ref), custom_call_target="tpu_custom_call" | custom-call | tf_op jit(solution)/shard_map/while/body/eval_jaxpr/while/body/pallas_call | solution.py:247
  180.1 25.3 %body.1 = f32[8,512]{1,0:T(8,128)S(1)} custom-call(f32[8,512]{1,0:T(8,128)} %copy.295.gain_ref, f32[8,256]{1,0:T(8,128)S(1)} %bitcast.552, f32[8,256]{1,0:T(8,128)S(1)} %bitcast.553, bf16[512,256]{1,0:T(8,128)(2,1)S(1)} %get-tuple-element.669.onehot_p_ref, bf16[512,256]{1,0:T(8,128)(2,1)S(1)} %get-tuple-element.670.onehot_q_ref, f32[1,1]{1,0:T(1,128)} %bitcast.547.damp_ref), custom_call_target="tpu_custom_call" | custom-call | tf_op jit(solution)/shard_map/while/body/eval_jaxpr/while/body/pallas_call | solution.py:247
  216.0 51.7 %while.44 = (s32[]{:T(128)}, f32[8,512]{1,0:T(8,128)S(1)}, s32[]{:T(128)}, f32[8,1,256]{2,0,1:T(8,128)S(1)}, f32[8,1,256]{2,0,1:T(8,128)S(1)}, /*index=5*/f32[]{...) while((s32[]{:T(128)}, f32[8,512]{1,0:T(8,128)S(1)}, s32[]{:T(128)}, ...), condition=%wide.region_4.6_spmd, body=%wide.region_3.5_spmd.sunk | while | flops 2 | bytes 32861 | solution.py:406
  216.6 25.1 %body.1 = f32[8,512]{1,0:T(8,128)S(1)} custom-call(f32[8,512]{1,0:T(8,128)} %copy.295.gain_ref, f32[8,256]{1,0:T(8,128)S(1)} %bitcast.552, f32[8,256]{1,0:T(8,128)S(1)} %bitcast.553, bf16[512,256]{1,0:T(8,128)(2,1)S(1)} %get-tuple-element.669.onehot_p_ref, bf16[512,256]{1,0:T(8,128)(2,1)S(1)} %get-tuple-element.670.onehot_q_ref, f32[1,1]{1,0:T(1,128)} %bitcast.547.damp_ref), custom_call_target="tpu_custom_call" | custom-call | tf_op jit(solution)/shard_map/while/body/eval_jaxpr/while/body/pallas_call | solution.py:247
  242.4 25.3 %body.1 = f32[8,512]{1,0:T(8,128)S(1)} custom-call(f32[8,512]{1,0:T(8,128)} %copy.295.gain_ref, f32[8,256]{1,0:T(8,128)S(1)} %bitcast.552, f32[8,256]{1,0:T(8,128)S(1)} %bitcast.553, bf16[512,256]{1,0:T(8,128)(2,1)S(1)} %get-tuple-element.669.onehot_p_ref, bf16[512,256]{1,0:T(8,128)(2,1)S(1)} %get-tuple-element.670.onehot_q_ref, f32[1,1]{1,0:T(1,128)} %bitcast.547.damp_ref), custom_call_target="tpu_custom_call" | custom-call | tf_op jit(solution)/shard_map/while/body/eval_jaxpr/while/body/pallas_call | solution.py:247
  (235 shorter events, 35.4 us)
Async XLA Ops:
  35.6 0.7 copy-start.4
  37.5 0.9 copy-start.1
  45.7 2.1 copy-start.3
  45.7 2.1 copy-start.2
  45.7 2.1 copy-start.5
  45.7 2.1 copy-start.6
  45.7 2.1 copy-start.7
  271.0 1.3 copy-start

commit v7 on v6

--- a/solution.py
+++ b/solution.py
@@ -107,9 +107,15 @@
     return [x[i : i + 1, :] for i in range(x.shape[0])]
 
 
+def model_rows(gain_parts, coher_now, onehot_p, onehot_q):
+    gain_p = rows_of(gather_cols(gain_parts, onehot_p))
+    gain_q = rows_of(gather_cols(gain_parts, onehot_q))
+    return matmul_rows(matmul_rows(gain_p, coher_now), adjoint_rows(gain_q))
+
+
 def round_kernel(
-    nb, nz, gain_ref, target_ref, coher_ref, onehot_p_ref, onehot_q_ref, damp_ref, o_ref,
-    pay, r1, r2, r3, s1, q1, s2, q2, s3, q3,
+    nb, nz, gain_ref, start_ref, residual_ref, coher_ref, onehot_p_ref, onehot_q_ref, damp_ref,
+    o_ref, res_out, pay, r1, r2, r3, s1, q1, s2, q2, s3, q3,
 ):
     mz = lax.axis_index("dir")
     mb = lax.axis_index("bl")
@@ -127,7 +133,11 @@
     gain_p = rows_of(gather_cols(parts, onehot_p_ref[...]))
     gain_q = rows_of(gather_cols(parts, onehot_q_ref[...]))
     coher_now = rows_of(coher_ref[...])
-    target = rows_of(target_ref[...])
+    start_model = model_rows(
+        split_three(start_ref[...]), coher_now, onehot_p_ref[...], onehot_q_ref[...]
+    )
+    residual_rows = rows_of(residual_ref[...])
+    target = [residual_rows[i] + start_model[i] for i in range(8)]
     z_rows = matmul_rows(coher_now, adjoint_rows(gain_q))
     y_rows = matmul_rows(adjoint_rows(coher_now), adjoint_rows(gain_p))
     zero_row = jnp.zeros_like(target[0])
@@ -212,7 +222,12 @@
         v / determinant
         for v in (diag_d, zeros_row, -cross_r, -cross_i, -cross_r, cross_i, diag_a, zeros_row)
     ]
-    o_ref[...] = jnp.concatenate(matmul_rows(numerator, inverse), 0)
+    updated = jnp.concatenate(matmul_rows(numerator, inverse), 0)
+    o_ref[...] = updated
+    final_model = model_rows(
+        split_three(updated), coher_now, onehot_p_ref[...], onehot_q_ref[...]
+    )
+    res_out[...] = jnp.concatenate([target[i] - final_model[i] for i in range(8)], 0)
 
 
 def matmul_rows(left, right):
@@ -240,15 +255,20 @@
     return [gram[0], gram[6], gram[2], gram[3]]
 
 
-def damped_round(gain_now, target, coher_now, onehot_p, onehot_q, damp_value, nb, nz):
+def damped_round(
+    gain_now, gain_start, residual, coher_now, onehot_p, onehot_q, damp_value, nb, nz
+):
     stations = gain_now.shape[1]
     per = (16 * stations) // (nb * 2 * 128)
     vmem = pl.BlockSpec(memory_space=pltpu.VMEM)
     return pl.pallas_call(
         functools.partial(round_kernel, nb, nz),
-        out_shape=jax.ShapeDtypeStruct(gain_now.shape, gain_now.dtype),
-        in_specs=[vmem] * 5 + [pl.BlockSpec(memory_space=pltpu.SMEM)],
-        out_specs=vmem,
+        out_shape=(
+            jax.ShapeDtypeStruct(gain_now.shape, gain_now.dtype),
+            jax.ShapeDtypeStruct(residual.shape, residual.dtype),
+        ),
+        in_specs=[vmem] * 6 + [pl.BlockSpec(memory_space=pltpu.SMEM)],
+        out_specs=(vmem, vmem),
         scratch_shapes=[
             pltpu.VMEM((nb, per, 2, 128), jnp.float32),
             pltpu.VMEM((nb, per, 2, 128), jnp.float32),
@@ -262,7 +282,7 @@
             pltpu.SemaphoreType.DMA((nb,)),
         ],
         compiler_params=pltpu.CompilerParams(collective_id=0, has_side_effects=True),
-    )(gain_now, target, coher_now, onehot_p, onehot_q, damp_value.reshape(1, 1))
+    )(gain_now, gain_start, residual, coher_now, onehot_p, onehot_q, damp_value.reshape(1, 1))
 
 
 def prologue_kernel(nb, nz, coh_ref, gain_ref, coh_out, gain_out, coh_buf, gain_buf, s1, q1, s2, q2):
@@ -389,23 +409,25 @@
     def sweep(step_index, state):
         gain_table, residual = state
         which = solve_order[step_index]
-        coher_now = lax.dynamic_index_in_dim(coher_all, which, 0, keepdims=False).astype(
+        coher_now = lax.dynamic_index_in_dim(coher_all, which, 0, keepdims=False)[:, 0, :].astype(
             jnp.float32
         )
         damp_value = damping[which].astype(jnp.float32) * damping_factor
         gain_start = gain_table[which]
-        target = residual + direction_model(gain_start, coher_now)
-
-        def iterate(round_index, gain_now):
+        residual_before = residual[:, 0, :]
+
+        def iterate(round_index, carry):
+            gain_now, _ = carry
             return damped_round(
-                gain_now, target[:, 0, :], coher_now[:, 0, :], onehot_p, onehot_q, damp_value,
-                groups, nz,
+                gain_now, gain_start, residual_before, coher_now, onehot_p, onehot_q,
+                damp_value, groups, nz,
             )
 
         rounds = jnp.clip(counts[which], 0, LM_ITERS)
-        gain_final = lax.fori_loop(0, rounds, iterate, gain_start)
-        residual = target - direction_model(gain_final, coher_now)
-        return (gain_table.at[which].set(gain_final), residual)
+        gain_final, residual_after = lax.fori_loop(
+            0, rounds, iterate, (gain_start, residual_before)
+        )
+        return (gain_table.at[which].set(gain_final), residual_after[:, None, :])
 
     gain_table, residual = lax.fori_loop(0, SOLVED, sweep, (start, first_residual))
     own_width = station_count // groups

time: 274 us -> 270 us (0.985)
  local copies, waits for them, and re-layouts: 39.9 us -> 31.9 us
  Pallas kernels: 206 us -> 213 us
    gather x32 -> x0, local copies, waits for them, and re-layouts: 12.7 us -> none  [the longest x16 6.35 us: direction_model(): gain_p = jnp.take(gain_now, stations[0], axis=1)[:, None, :]]
    pallas_call x7, Pallas kernels: 176 us -> 183 us  [damped_round(): pl.pallas_call(functools.partial(round_kernel, nb, nz), out_shape=(jax.Sh...]
    while x15 -> x19, local copies, waits for them, and re-layouts: 4.75 us -> 9.45 us
where the time goes in v7:
time: 270 us; the launch traced here: 268 us
  Pallas kernels  213 us (79%)
  local copies, waits for them, and re-layouts  31.9 us (12%)
  loops' own time  13.4 us (5%)
  other arithmetic  9.25 us (3%)
    pallas_call x7, Pallas kernels, damped_round(): pl.pallas_call(functools.partial(round_kernel, nb, nz), out_shape=(jax.Sh...  183 us
    pallas_call x1, Pallas kernels, exchange_inputs(): pl.pallas_call(functools.partial(prologue_kernel, nb, nz), out_shape=(jax...  30.2 us
    another operation x1, loops' own time, on_device(): lax.fori_loop(0, SOLVED, sweep, (start, first_residual))  13.2 us
    while x19, local copies, waits for them, and re-layouts  9.45 us

profile of v7, /device:TPU:1, one launch (start us, length us, event | category | flops | bytes accessed | tf_op | source)
XLA Modules:
  0.0 268.4 jit_solution(3196888976119322941)
XLA Ops:
  0.6 1.6 copy.95
  2.2 1.5 copy.64.gain_ref
  3.7 30.2 %shard_map.86 = (bf16[16,16,256]{2,1,0:T(8,128)(2,1)S(1)}, f32[32,32,128]{2,1,0:T(8,128)}) custom-call(bf16[16,16,256]{2,1,0:T(8,128)(2,1)} %bitcast.259, f32[32,128]{1,0:T(8,128)} %copy.64.gain_ref), custom_call_target="tpu_custom_call" | custom-call | tf_op jit(solution)/shard_map/pallas_call | solution.py:354
  33.9 1.6 copy.65
  36.2 1.2 copy_add_fusion
  37.5 0.9 copy.80
  38.5 2.0 gather_fusion.1
  40.5 1.6 copy.70
  42.1 2.0 gather_fusion
  44.1 1.6 copy.68
  47.8 218.7 %while.49 = (s32[]{:T(128)}, f32[32,8,512]{2,1,0:T(8,128)S(1)}, f32[8,1,256]{2,0,1:T(8,128)S(1)}, s32[32]{0:T(128)S(1)}, s32[32]{0:T(128)S(1)}, /*index=5*/s32[3...) while((s32[]{:T(128)}, f32[32,8,512]{2,1,0:T(8,128)S(1)}, ...), condition=%wide.region_5.7_spmd.clone, body=%wide.region_1.6_spmd.clone.sunk | while | flops 530460 | bytes 719366 | solution.py:432
  53.6 53.2 %while.50 = (s32[]{:T(128)}, f32[8,512]{1,0:T(8,128)S(1)}, f32[8,256]{1,0:T(8,128)}, s32[]{:T(128)}, f32[]{:T(128)}, /*index=5*/f32[8,512]{1,0:T(8,128)S(1)}, f3...) while((s32[]{:T(128)}, f32[8,512]{1,0:T(8,128)S(1)}, ...), condition=%wide.region_4.5_spmd, body=%wide.region_3.4_spmd.sunk | while | flops 2 | bytes 32877 | solution.py:427
  54.2 25.9 %body.1 = (f32[8,512]{1,0:T(8,128)S(1)}, f32[8,256]{1,0:T(8,128)}) custom-call(f32[8,512]{1,0:T(8,128)} %copy.125.gain_ref, f32[8,512]{1,0:T(8,128)S(1)} %get-tuple-element.569.start_ref, f32[8,256]{1,0:T(8,128)S(1)} %get-tuple-element.570.residual_ref, f32[8,256]{1,0:T(8,128)S(1)} %get-tuple-element.571.coher_ref, ...), custom_call_target="tpu_custom_call" | custom-call | tf_op jit(solution)/shard_map/while/body/eval_jaxpr/while/body/pallas_call | solution.py:264
  80.8 26.0 %body.1 = (f32[8,512]{1,0:T(8,128)S(1)}, f32[8,256]{1,0:T(8,128)}) custom-call(f32[8,512]{1,0:T(8,128)} %copy.125.gain_ref, f32[8,512]{1,0:T(8,128)S(1)} %get-tuple-element.569.start_ref, f32[8,256]{1,0:T(8,128)S(1)} %get-tuple-element.570.residual_ref, f32[8,256]{1,0:T(8,128)S(1)} %get-tuple-element.571.coher_ref, ...), custom_call_target="tpu_custom_call" | custom-call | tf_op jit(solution)/shard_map/while/body/eval_jaxpr/while/body/pallas_call | solution.py:264
  106.8 0.7 and_reduce_fusion.2
  114.7 26.8 %while.50 = (s32[]{:T(128)}, f32[8,512]{1,0:T(8,128)S(1)}, f32[8,256]{1,0:T(8,128)}, s32[]{:T(128)}, f32[]{:T(128)}, /*index=5*/f32[8,512]{1,0:T(8,128)S(1)}, f3...) while((s32[]{:T(128)}, f32[8,512]{1,0:T(8,128)S(1)}, ...), condition=%wide.region_4.5_spmd, body=%wide.region_3.4_spmd.sunk | while | flops 2 | bytes 32877 | solution.py:427
  115.3 26.1 %body.1 = (f32[8,512]{1,0:T(8,128)S(1)}, f32[8,256]{1,0:T(8,128)}) custom-call(f32[8,512]{1,0:T(8,128)} %copy.125.gain_ref, f32[8,512]{1,0:T(8,128)S(1)} %get-tuple-element.569.start_ref, f32[8,256]{1,0:T(8,128)S(1)} %get-tuple-element.570.residual_ref, f32[8,256]{1,0:T(8,128)S(1)} %get-tuple-element.571.coher_ref, ...), custom_call_target="tpu_custom_call" | custom-call | tf_op jit(solution)/shard_map/while/body/eval_jaxpr/while/body/pallas_call | solution.py:264
  149.3 53.7 %while.50 = (s32[]{:T(128)}, f32[8,512]{1,0:T(8,128)S(1)}, f32[8,256]{1,0:T(8,128)}, s32[]{:T(128)}, f32[]{:T(128)}, /*index=5*/f32[8,512]{1,0:T(8,128)S(1)}, f3...) while((s32[]{:T(128)}, f32[8,512]{1,0:T(8,128)S(1)}, ...), condition=%wide.region_4.5_spmd, body=%wide.region_3.4_spmd.sunk | while | flops 2 | bytes 32877 | solution.py:427
  150.0 26.2 %body.1 = (f32[8,512]{1,0:T(8,128)S(1)}, f32[8,256]{1,0:T(8,128)}) custom-call(f32[8,512]{1,0:T(8,128)} %copy.125.gain_ref, f32[8,512]{1,0:T(8,128)S(1)} %get-tuple-element.569.start_ref, f32[8,256]{1,0:T(8,128)S(1)} %get-tuple-element.570.residual_ref, f32[8,256]{1,0:T(8,128)S(1)} %get-tuple-element.571.coher_ref, ...), custom_call_target="tpu_custom_call" | custom-call | tf_op jit(solution)/shard_map/while/body/eval_jaxpr/while/body/pallas_call | solution.py:264
  176.8 26.2 %body.1 = (f32[8,512]{1,0:T(8,128)S(1)}, f32[8,256]{1,0:T(8,128)}) custom-call(f32[8,512]{1,0:T(8,128)} %copy.125.gain_ref, f32[8,512]{1,0:T(8,128)S(1)} %get-tuple-element.569.start_ref, f32[8,256]{1,0:T(8,128)S(1)} %get-tuple-element.570.residual_ref, f32[8,256]{1,0:T(8,128)S(1)} %get-tuple-element.571.coher_ref, ...), custom_call_target="tpu_custom_call" | custom-call | tf_op jit(solution)/shard_map/while/body/eval_jaxpr/while/body/pallas_call | solution.py:264
  210.9 53.5 %while.50 = (s32[]{:T(128)}, f32[8,512]{1,0:T(8,128)S(1)}, f32[8,256]{1,0:T(8,128)}, s32[]{:T(128)}, f32[]{:T(128)}, /*index=5*/f32[8,512]{1,0:T(8,128)S(1)}, f3...) while((s32[]{:T(128)}, f32[8,512]{1,0:T(8,128)S(1)}, ...), condition=%wide.region_4.5_spmd, body=%wide.region_3.4_spmd.sunk | while | flops 2 | bytes 32877 | solution.py:427
  211.5 26.1 %body.1 = (f32[8,512]{1,0:T(8,128)S(1)}, f32[8,256]{1,0:T(8,128)}) custom-call(f32[8,512]{1,0:T(8,128)} %copy.125.gain_ref, f32[8,512]{1,0:T(8,128)S(1)} %get-tuple-element.569.start_ref, f32[8,256]{1,0:T(8,128)S(1)} %get-tuple-element.570.residual_ref, f32[8,256]{1,0:T(8,128)S(1)} %get-tuple-element.571.coher_ref, ...), custom_call_target="tpu_custom_call" | custom-call | tf_op jit(solution)/shard_map/while/body/eval_jaxpr/while/body/pallas_call | solution.py:264
  238.2 26.2 %body.1 = (f32[8,512]{1,0:T(8,128)S(1)}, f32[8,256]{1,0:T(8,128)}) custom-call(f32[8,512]{1,0:T(8,128)} %copy.125.gain_ref, f32[8,512]{1,0:T(8,128)S(1)} %get-tuple-element.569.start_ref, f32[8,256]{1,0:T(8,128)S(1)} %get-tuple-element.570.residual_ref, f32[8,256]{1,0:T(8,128)S(1)} %get-tuple-element.571.coher_ref, ...), custom_call_target="tpu_custom_call" | custom-call | tf_op jit(solution)/shard_map/while/body/eval_jaxpr/while/body/pallas_call | solution.py:264
  264.4 0.7 and_reduce_fusion.2
  (90 shorter events, 25.7 us)
Async XLA Ops:
  35.6 0.7 copy-start.3
  37.5 0.9 copy-start.2
  45.7 2.1 copy-start.1
  45.7 2.1 copy-start
  45.7 2.1 copy-start.4
  45.7 2.1 copy-start.5
  45.7 2.1 copy-start.6

commit v8 on v7

--- a/solution.py
+++ b/solution.py
@@ -114,7 +114,7 @@
 
 
 def round_kernel(
-    nb, nz, gain_ref, start_ref, residual_ref, coher_ref, onehot_p_ref, onehot_q_ref, damp_ref,
+    nb, nz, rounds, gain_ref, start_ref, residual_ref, coher_ref, onehot_p_ref, onehot_q_ref, damp_ref,
     o_ref, res_out, pay, r1, r2, r3, s1, q1, s2, q2, s3, q3,
 ):
     mz = lax.axis_index("dir")
@@ -128,50 +128,25 @@
     for p in z_peers:
         pl.semaphore_signal(barrier, 1, device_id=(mb, p), device_id_type=MESH_ID)
 
-    gain_now = gain_ref[...]
-    parts = split_three(gain_now)
-    gain_p = rows_of(gather_cols(parts, onehot_p_ref[...]))
-    gain_q = rows_of(gather_cols(parts, onehot_q_ref[...]))
     coher_now = rows_of(coher_ref[...])
-    start_model = model_rows(
-        split_three(start_ref[...]), coher_now, onehot_p_ref[...], onehot_q_ref[...]
-    )
+    onehot_p = onehot_p_ref[...]
+    onehot_q = onehot_q_ref[...]
+    start_model = model_rows(split_three(start_ref[...]), coher_now, onehot_p, onehot_q)
     residual_rows = rows_of(residual_ref[...])
     target = [residual_rows[i] + start_model[i] for i in range(8)]
-    z_rows = matmul_rows(coher_now, adjoint_rows(gain_q))
-    y_rows = matmul_rows(adjoint_rows(coher_now), adjoint_rows(gain_p))
-    zero_row = jnp.zeros_like(target[0])
-    leading = (
-        matmul_rows(target, adjoint_rows(z_rows))
-        + gram_rows(matmul_rows(z_rows, adjoint_rows(z_rows)))
-        + [zero_row] * 4
-    )
-    second = (
-        matmul_rows(adjoint_rows(target), adjoint_rows(y_rows))
-        + gram_rows(matmul_rows(y_rows, adjoint_rows(y_rows)))
-        + [zero_row] * 4
-    )
-    sums = scatter_cols(jnp.concatenate(leading, 0), onehot_p_ref[...]) + scatter_cols(
-        jnp.concatenate(second, 0), onehot_q_ref[...]
-    )
-    groups = sums.shape[1] // 128
-    pairs = sums.shape[0] // 2
+    damp_value = damp_ref[0, 0]
+    groups = None
+    pairs = None
     per = pay.shape[1]
-    for g in range(groups):
-        for h in range(pairs):
-            slab = g * pairs + h
-            pay[slab // per, slab % per] = sums[2 * h : 2 * h + 2, 128 * g : 128 * g + 128]
-
-    pl.semaphore_wait(barrier, (nz - 1) + (nb - 1))
-
-    def exchange(peers, src_of, buf, me, send_sems, recv_sems, device_of):
+
+    def exchange(peers, src_of, buf, me, send_sems, recv_sems, device_of, r):
         sent = []
         for p in peers:
             c = pltpu.make_async_remote_copy(
                 src_ref=src_of(p),
-                dst_ref=buf.at[me],
-                send_sem=send_sems.at[p],
-                recv_sem=recv_sems.at[me],
+                dst_ref=buf.at[r, me],
+                send_sem=send_sems.at[r, p],
+                recv_sem=recv_sems.at[r, me],
                 device_id=device_of(p),
                 device_id_type=MESH_ID,
             )
@@ -179,54 +154,91 @@
             sent.append(c)
         for p in peers:
             pltpu.make_async_remote_copy(
-                src_ref=buf.at[p],
-                dst_ref=buf.at[p],
-                send_sem=send_sems.at[p],
-                recv_sem=recv_sems.at[p],
+                src_ref=buf.at[r, p],
+                dst_ref=buf.at[r, p],
+                send_sem=send_sems.at[r, p],
+                recv_sem=recv_sems.at[r, p],
                 device_id=device_of(p),
                 device_id_type=MESH_ID,
             ).wait_recv()
         for c in sent:
             c.wait_send()
 
-    exchange(b_peers, lambda p: pay.at[p], r1, mb, s1, q1, lambda p: (p, mz))
-    own = pay[mb]
-    for p in b_peers:
-        own = own + r1[p]
-    r2[mz] = own
-    exchange(z_peers, lambda p: r2.at[mz], r2, mz, s2, q2, lambda p: (mb, p))
-    total = r2[mz]
-    for p in z_peers:
-        total = total + r2[p]
-    r3[mb] = total
-    exchange(b_peers, lambda p: r3.at[mb], r3, mb, s3, q3, lambda p: (p, mz))
-
-    gathered = []
-    for h in range(pairs):
-        for t in range(2):
-            pieces = []
-            for g in range(groups):
+    def local_sums(gain_now):
+        parts = split_three(gain_now)
+        gain_p = rows_of(gather_cols(parts, onehot_p))
+        gain_q = rows_of(gather_cols(parts, onehot_q))
+        z_rows = matmul_rows(coher_now, adjoint_rows(gain_q))
+        y_rows = matmul_rows(adjoint_rows(coher_now), adjoint_rows(gain_p))
+        zero_row = jnp.zeros_like(target[0])
+        leading = (
+            matmul_rows(target, adjoint_rows(z_rows))
+            + gram_rows(matmul_rows(z_rows, adjoint_rows(z_rows)))
+            + [zero_row] * 4
+        )
+        second = (
+            matmul_rows(adjoint_rows(target), adjoint_rows(y_rows))
+            + gram_rows(matmul_rows(y_rows, adjoint_rows(y_rows)))
+            + [zero_row] * 4
+        )
+        sums = scatter_cols(jnp.concatenate(leading, 0), onehot_p) + scatter_cols(
+            jnp.concatenate(second, 0), onehot_q
+        )
+        groups = sums.shape[1] // 128
+        pairs = sums.shape[0] // 2
+        for g in range(groups):
+            for h in range(pairs):
                 slab = g * pairs + h
-                pieces.append(r3[slab // per, slab % per, t : t + 1, :])
-            gathered.append(jnp.concatenate(pieces, 1))
-    damp_value = damp_ref[0, 0]
-    gain_rows = rows_of(gain_now)
-    numerator = [gathered[i] + damp_value * gain_rows[i] for i in range(8)]
-    diag_a = gathered[8] + damp_value
-    diag_d = gathered[9] + damp_value
-    cross_r = gathered[10]
-    cross_i = gathered[11]
-    determinant = diag_a * diag_d - cross_r * cross_r - cross_i * cross_i
-    zeros_row = jnp.zeros_like(determinant)
-    inverse = [
-        v / determinant
-        for v in (diag_d, zeros_row, -cross_r, -cross_i, -cross_r, cross_i, diag_a, zeros_row)
-    ]
-    updated = jnp.concatenate(matmul_rows(numerator, inverse), 0)
-    o_ref[...] = updated
-    final_model = model_rows(
-        split_three(updated), coher_now, onehot_p_ref[...], onehot_q_ref[...]
-    )
+                pay[slab // per, slab % per] = sums[2 * h : 2 * h + 2, 128 * g : 128 * g + 128]
+        return groups, pairs
+
+    def all_reduce(r):
+        exchange(b_peers, lambda p: pay.at[p], r1, mb, s1, q1, lambda p: (p, mz), r)
+        own = pay[mb]
+        for p in b_peers:
+            own = own + r1[r, p]
+        r2[r, mz] = own
+        exchange(z_peers, lambda p: r2.at[r, mz], r2, mz, s2, q2, lambda p: (mb, p), r)
+        total = r2[r, mz]
+        for p in z_peers:
+            total = total + r2[r, p]
+        r3[r, mb] = total
+        exchange(b_peers, lambda p: r3.at[r, mb], r3, mb, s3, q3, lambda p: (p, mz), r)
+
+    def solve(gain_now, groups, pairs, r):
+        gathered = []
+        for h in range(pairs):
+            for t in range(2):
+                pieces = []
+                for g in range(groups):
+                    slab = g * pairs + h
+                    pieces.append(r3[r, slab // per, slab % per, t : t + 1, :])
+                gathered.append(jnp.concatenate(pieces, 1))
+        gain_rows = rows_of(gain_now)
+        numerator = [gathered[i] + damp_value * gain_rows[i] for i in range(8)]
+        diag_a = gathered[8] + damp_value
+        diag_d = gathered[9] + damp_value
+        cross_r = gathered[10]
+        cross_i = gathered[11]
+        determinant = diag_a * diag_d - cross_r * cross_r - cross_i * cross_i
+        zeros_row = jnp.zeros_like(determinant)
+        inverse = [
+            v / determinant
+            for v in (diag_d, zeros_row, -cross_r, -cross_i, -cross_r, cross_i, diag_a, zeros_row)
+        ]
+        return jnp.concatenate(matmul_rows(numerator, inverse), 0)
+
+    gain_now = gain_ref[...]
+    groups, pairs = local_sums(gain_now)
+    pl.semaphore_wait(barrier, (nz - 1) + (nb - 1))
+    all_reduce(0)
+    gain_now = solve(gain_now, groups, pairs, 0)
+    for r in range(1, rounds):
+        local_sums(gain_now)
+        all_reduce(r)
+        gain_now = solve(gain_now, groups, pairs, r)
+    o_ref[...] = gain_now
+    final_model = model_rows(split_three(gain_now), coher_now, onehot_p, onehot_q)
     res_out[...] = jnp.concatenate([target[i] - final_model[i] for i in range(8)], 0)
 
 
@@ -255,14 +267,14 @@
     return [gram[0], gram[6], gram[2], gram[3]]
 
 
-def damped_round(
-    gain_now, gain_start, residual, coher_now, onehot_p, onehot_q, damp_value, nb, nz
+def damped_rounds(
+    rounds, gain_now, gain_start, residual, coher_now, onehot_p, onehot_q, damp_value, nb, nz
 ):
     stations = gain_now.shape[1]
     per = (16 * stations) // (nb * 2 * 128)
     vmem = pl.BlockSpec(memory_space=pltpu.VMEM)
     return pl.pallas_call(
-        functools.partial(round_kernel, nb, nz),
+        functools.partial(round_kernel, nb, nz, rounds),
         out_shape=(
             jax.ShapeDtypeStruct(gain_now.shape, gain_now.dtype),
             jax.ShapeDtypeStruct(residual.shape, residual.dtype),
@@ -271,17 +283,17 @@
         out_specs=(vmem, vmem),
         scratch_shapes=[
             pltpu.VMEM((nb, per, 2, 128), jnp.float32),
-            pltpu.VMEM((nb, per, 2, 128), jnp.float32),
-            pltpu.VMEM((nz, per, 2, 128), jnp.float32),
-            pltpu.VMEM((nb, per, 2, 128), jnp.float32),
-            pltpu.SemaphoreType.DMA((nb,)),
-            pltpu.SemaphoreType.DMA((nb,)),
-            pltpu.SemaphoreType.DMA((nz,)),
-            pltpu.SemaphoreType.DMA((nz,)),
-            pltpu.SemaphoreType.DMA((nb,)),
-            pltpu.SemaphoreType.DMA((nb,)),
+            pltpu.VMEM((rounds, nb, per, 2, 128), jnp.float32),
+            pltpu.VMEM((rounds, nz, per, 2, 128), jnp.float32),
+            pltpu.VMEM((rounds, nb, per, 2, 128), jnp.float32),
+            pltpu.SemaphoreType.DMA((rounds, nb)),
+            pltpu.SemaphoreType.DMA((rounds, nb)),
+            pltpu.SemaphoreType.DMA((rounds, nz)),
+            pltpu.SemaphoreType.DMA((rounds, nz)),
+            pltpu.SemaphoreType.DMA((rounds, nb)),
+            pltpu.SemaphoreType.DMA((rounds, nb)),
         ],
-        compiler_params=pltpu.CompilerParams(collective_id=0, has_side_effects=True),
+        compiler_params=pltpu.CompilerParams(collective_id=2 * rounds, has_side_effects=True),
     )(gain_now, gain_start, residual, coher_now, onehot_p, onehot_q, damp_value.reshape(1, 1))
 
 
@@ -416,16 +428,20 @@
         gain_start = gain_table[which]
         residual_before = residual[:, 0, :]
 
-        def iterate(round_index, carry):
-            gain_now, _ = carry
-            return damped_round(
-                gain_now, gain_start, residual_before, coher_now, onehot_p, onehot_q,
-                damp_value, groups, nz,
-            )
+        def run(rounds):
+            def branch(operands):
+                if rounds == 0:
+                    return (gain_start, residual_before)
+                return damped_rounds(
+                    rounds, gain_start, gain_start, residual_before, coher_now, onehot_p,
+                    onehot_q, damp_value, groups, nz,
+                )
+
+            return branch
 
         rounds = jnp.clip(counts[which], 0, LM_ITERS)
-        gain_final, residual_after = lax.fori_loop(
-            0, rounds, iterate, (gain_start, residual_before)
+        gain_final, residual_after = lax.switch(
+            rounds, [run(r) for r in range(LM_ITERS + 1)], None
         )
         return (gain_table.at[which].set(gain_final), residual_after[:, None, :])
 

time: 270 us -> 245 us (0.907)
  Pallas kernels: 213 us -> 191 us
  local copies, waits for them, and re-layouts: 31.9 us -> 27.2 us
    pallas_call x7 -> x4, Pallas kernels: 183 us -> 161 us  [damped_rounds(): pl.pallas_call(functools.partial(round_kernel, nb, nz, rounds), out_shape...]
    while x19 -> x0, local copies, waits for them, and re-layouts: 9.45 us -> none
    cond x0 -> x8, local copies, waits for them, and re-layouts: none -> 4.82 us
where the time goes in v8:
time: 245 us; the launch traced here: 244 us
  Pallas kernels  191 us (78%)
  local copies, waits for them, and re-layouts  27.2 us (11%)
  loops' own time  13.1 us (5%)
  other arithmetic  11.6 us (5%)
    pallas_call x4, Pallas kernels, damped_rounds(): pl.pallas_call(functools.partial(round_kernel, nb, nz, rounds), out_shape...  161 us
    pallas_call x1, Pallas kernels, exchange_inputs(): pl.pallas_call(functools.partial(prologue_kernel, nb, nz), out_shape=(jax...  30.2 us
    another operation x1, loops' own time, on_device(): lax.fori_loop(0, SOLVED, sweep, (start, first_residual))  10.8 us

profile of v8, /device:TPU:1, one launch (start us, length us, event | category | flops | bytes accessed | tf_op | source)
XLA Modules:
  0.0 244.1 jit_solution(2397180278024215106)
XLA Ops:
  0.6 1.6 copy.95
  2.2 1.5 copy.64.gain_ref
  3.7 30.2 %shard_map.86 = (bf16[16,16,256]{2,1,0:T(8,128)(2,1)S(1)}, f32[32,32,128]{2,1,0:T(8,128)}) custom-call(bf16[16,16,256]{2,1,0:T(8,128)(2,1)} %bitcast.257, f32[32,128]{1,0:T(8,128)} %copy.64.gain_ref), custom_call_target="tpu_custom_call" | custom-call | tf_op jit(solution)/shard_map/pallas_call | solution.py:366
  33.9 1.6 copy.65
  36.2 1.2 copy_add_fusion
  37.5 0.9 copy.80
  38.4 2.0 gather_fusion.1
  40.4 1.6 copy.70
  42.1 2.0 gather_fusion
  44.1 1.6 copy.68
  47.8 194.4 %while.19 = (s32[]{:T(128)}, f32[32,8,512]{2,1,0:T(8,128)S(1)}, f32[8,1,256]{2,0,1:T(8,128)S(1)}, s32[32]{0:T(128)S(1)}, s32[32]{0:T(128)S(1)}, /*index=5*/bf16[...) while((s32[]{:T(128)}, f32[32,8,512]{2,1,0:T(8,128)S(1)}, ...), condition=%wide.region_6.8_spmd.clone, body=%wide.region_1.7_spmd.clone.sunk | while | flops 530459 | bytes 670145 | solution.py:448
  51.9 49.1 %conditional.3 = ((f32[8,512]{1,0:T(8,128)S(1)}, f32[8,256]{1,0:T(8,128)S(1)})) conditional(s32[]{:T(128)} %bitcast.247, (f32[8,512]{1,0:T(8,128)S(1)}, f32[8,256]{1,0:T(8,128)S(1)}) %tuple.148, (bf16[32,8,1,256]{3,1,2,0:T(8,128)(2,1)S(1)}, s32[]{:T(128)}, s32[32]{0:T(128)S(1)}, f32[8,512]{1,0:T(8,128)S(1)}, f32[8,256]{1,0:T(8,128)S(1)}, ...), branch_computations={%region_3.4_spmd, %region_4.5_spmd, %region_5.6_spmd} | conditional | flops 2050 | bytes 61484 | solution.py:443
  54.9 46.1 %branch_2_fun.3 = (f32[8,512]{1,0:T(8,128)S(1)}, f32[8,256]{1,0:T(8,128)S(1)}) custom-call(f32[8,512]{1,0:T(8,128)} %copy.124.gain_ref.start_ref, f32[8,512]{1,0:T(8,128)} %copy.124.gain_ref.start_ref, f32[8,256]{1,0:T(8,128)} %copy.122.residual_ref, f32[8,256]{1,0:T(8,128)} %bitcast_convert_fusion.1.coher_ref, ...), custom_call_target="tpu_custom_call" | custom-call | tf_op jit(solution)/shard_map/while/body/eval_jaxpr/cond/branch_2_fun/pallas_call | solution.py:276
  101.0 0.7 and_reduce_fusion.2
  101.8 0.7 fusion.15
  106.4 45.4 %conditional.3 = ((f32[8,512]{1,0:T(8,128)S(1)}, f32[8,256]{1,0:T(8,128)S(1)})) conditional(s32[]{:T(128)} %bitcast.247, (f32[8,512]{1,0:T(8,128)S(1)}, f32[8,256]{1,0:T(8,128)S(1)}) %tuple.148, (bf16[32,8,1,256]{3,1,2,0:T(8,128)(2,1)S(1)}, s32[]{:T(128)}, s32[32]{0:T(128)S(1)}, f32[8,512]{1,0:T(8,128)S(1)}, f32[8,256]{1,0:T(8,128)S(1)}, ...), branch_computations={%region_3.4_spmd, %region_4.5_spmd, %region_5.6_spmd} | conditional | flops 2050 | bytes 61484 | solution.py:443
  109.3 42.5 %branch_2_fun.3 = (f32[8,512]{1,0:T(8,128)S(1)}, f32[8,256]{1,0:T(8,128)S(1)}) custom-call(f32[8,512]{1,0:T(8,128)} %copy.124.gain_ref.start_ref, f32[8,512]{1,0:T(8,128)} %copy.124.gain_ref.start_ref, f32[8,256]{1,0:T(8,128)} %copy.122.residual_ref, f32[8,256]{1,0:T(8,128)} %bitcast_convert_fusion.1.coher_ref, ...), custom_call_target="tpu_custom_call" | custom-call | tf_op jit(solution)/shard_map/while/body/eval_jaxpr/cond/branch_2_fun/pallas_call | solution.py:276
  151.8 0.7 and_reduce_fusion.2
  157.2 29.0 %conditional.3 = ((f32[8,512]{1,0:T(8,128)S(1)}, f32[8,256]{1,0:T(8,128)S(1)})) conditional(s32[]{:T(128)} %bitcast.247, (f32[8,512]{1,0:T(8,128)S(1)}, f32[8,256]{1,0:T(8,128)S(1)}) %tuple.148, (bf16[32,8,1,256]{3,1,2,0:T(8,128)(2,1)S(1)}, s32[]{:T(128)}, s32[32]{0:T(128)S(1)}, f32[8,512]{1,0:T(8,128)S(1)}, f32[8,256]{1,0:T(8,128)S(1)}, ...), branch_computations={%region_3.4_spmd, %region_4.5_spmd, %region_5.6_spmd} | conditional | flops 2050 | bytes 61484 | solution.py:443
  160.1 26.0 %branch_1_fun.3 = (f32[8,512]{1,0:T(8,128)S(1)}, f32[8,256]{1,0:T(8,128)S(1)}) custom-call(f32[8,512]{1,0:T(8,128)} %copy.123.gain_ref.start_ref, f32[8,512]{1,0:T(8,128)} %copy.123.gain_ref.start_ref, f32[8,256]{1,0:T(8,128)} %copy.120.residual_ref, f32[8,256]{1,0:T(8,128)} %bitcast_convert_fusion.coher_ref, ...), custom_call_target="tpu_custom_call" | custom-call | tf_op jit(solution)/shard_map/while/body/eval_jaxpr/cond/branch_1_fun/pallas_call | solution.py:276
  186.2 0.7 and_reduce_fusion.2
  191.5 49.4 %conditional.3 = ((f32[8,512]{1,0:T(8,128)S(1)}, f32[8,256]{1,0:T(8,128)S(1)})) conditional(s32[]{:T(128)} %bitcast.247, (f32[8,512]{1,0:T(8,128)S(1)}, f32[8,256]{1,0:T(8,128)S(1)}) %tuple.148, (bf16[32,8,1,256]{3,1,2,0:T(8,128)(2,1)S(1)}, s32[]{:T(128)}, s32[32]{0:T(128)S(1)}, f32[8,512]{1,0:T(8,128)S(1)}, f32[8,256]{1,0:T(8,128)S(1)}, ...), branch_computations={%region_3.4_spmd, %region_4.5_spmd, %region_5.6_spmd} | conditional | flops 2050 | bytes 61484 | solution.py:443
  194.4 46.4 %branch_2_fun.3 = (f32[8,512]{1,0:T(8,128)S(1)}, f32[8,256]{1,0:T(8,128)S(1)}) custom-call(f32[8,512]{1,0:T(8,128)} %copy.124.gain_ref.start_ref, f32[8,512]{1,0:T(8,128)} %copy.124.gain_ref.start_ref, f32[8,256]{1,0:T(8,128)} %copy.122.residual_ref, f32[8,256]{1,0:T(8,128)} %bitcast_convert_fusion.1.coher_ref, ...), custom_call_target="tpu_custom_call" | custom-call | tf_op jit(solution)/shard_map/while/body/eval_jaxpr/cond/branch_2_fun/pallas_call | solution.py:276
  240.9 0.7 and_reduce_fusion.2
  (76 shorter events, 21.3 us)
Async XLA Ops:
  35.6 0.7 copy-start.3
  37.4 0.9 copy-start.2
  45.7 2.1 copy-start.1
  45.7 2.1 copy-start
  45.7 2.1 copy-start.4
  45.7 2.1 copy-start.5
  45.7 2.1 copy-start.6

commit v9 on v8

--- a/solution.py
+++ b/solution.py
@@ -114,8 +114,8 @@
 
 
 def round_kernel(
-    nb, nz, rounds, gain_ref, start_ref, residual_ref, coher_ref, onehot_p_ref, onehot_q_ref, damp_ref,
-    o_ref, res_out, pay, r1, r2, r3, s1, q1, s2, q2, s3, q3,
+    nb, nz, rounds, which_ref, damp_ref, table_ref, residual_ref, coher_ref, onehot_p_ref,
+    onehot_q_ref, o_ref, res_out, pay, r1, r2, r3, s1, q1, s2, q2, s3, q3,
 ):
     mz = lax.axis_index("dir")
     mb = lax.axis_index("bl")
@@ -128,10 +128,12 @@
     for p in z_peers:
         pl.semaphore_signal(barrier, 1, device_id=(mb, p), device_id_type=MESH_ID)
 
-    coher_now = rows_of(coher_ref[...])
+    which = which_ref[0]
+    gain_start = table_ref[which]
+    coher_now = rows_of(coher_ref[which].astype(jnp.float32))
     onehot_p = onehot_p_ref[...]
     onehot_q = onehot_q_ref[...]
-    start_model = model_rows(split_three(start_ref[...]), coher_now, onehot_p, onehot_q)
+    start_model = model_rows(split_three(gain_start), coher_now, onehot_p, onehot_q)
     residual_rows = rows_of(residual_ref[...])
     target = [residual_rows[i] + start_model[i] for i in range(8)]
     damp_value = damp_ref[0, 0]
@@ -228,7 +230,7 @@
         ]
         return jnp.concatenate(matmul_rows(numerator, inverse), 0)
 
-    gain_now = gain_ref[...]
+    gain_now = gain_start
     groups, pairs = local_sums(gain_now)
     pl.semaphore_wait(barrier, (nz - 1) + (nb - 1))
     all_reduce(0)
@@ -268,18 +270,19 @@
 
 
 def damped_rounds(
-    rounds, gain_now, gain_start, residual, coher_now, onehot_p, onehot_q, damp_value, nb, nz
+    rounds, which, damp_value, gain_table, residual, coher_all, onehot_p, onehot_q, nb, nz
 ):
-    stations = gain_now.shape[1]
+    stations = gain_table.shape[2]
     per = (16 * stations) // (nb * 2 * 128)
     vmem = pl.BlockSpec(memory_space=pltpu.VMEM)
+    smem = pl.BlockSpec(memory_space=pltpu.SMEM)
     return pl.pallas_call(
         functools.partial(round_kernel, nb, nz, rounds),
         out_shape=(
-            jax.ShapeDtypeStruct(gain_now.shape, gain_now.dtype),
+            jax.ShapeDtypeStruct(gain_table.shape[1:], gain_table.dtype),
             jax.ShapeDtypeStruct(residual.shape, residual.dtype),
         ),
-        in_specs=[vmem] * 6 + [pl.BlockSpec(memory_space=pltpu.SMEM)],
+        in_specs=[smem, smem] + [vmem] * 5,
         out_specs=(vmem, vmem),
         scratch_shapes=[
             pltpu.VMEM((nb, per, 2, 128), jnp.float32),
@@ -294,7 +297,10 @@
             pltpu.SemaphoreType.DMA((rounds, nb)),
         ],
         compiler_params=pltpu.CompilerParams(collective_id=2 * rounds, has_side_effects=True),
-    )(gain_now, gain_start, residual, coher_now, onehot_p, onehot_q, damp_value.reshape(1, 1))
+    )(
+        which.reshape(1), damp_value.reshape(1, 1), gain_table, residual, coher_all, onehot_p,
+        onehot_q,
+    )
 
 
 def prologue_kernel(nb, nz, coh_ref, gain_ref, coh_out, gain_out, coh_buf, gain_buf, s1, q1, s2, q2):
@@ -418,23 +424,21 @@
         gain_q = jnp.take(gain_now, stations[1], axis=1)[:, None, :]
         return apply_gains(gain_p, coher_now, gain_q)
 
+    coher_rows = coher_all.reshape(coher_all.shape[0], 8, coher_all.shape[3])
+
     def sweep(step_index, state):
         gain_table, residual = state
         which = solve_order[step_index]
-        coher_now = lax.dynamic_index_in_dim(coher_all, which, 0, keepdims=False)[:, 0, :].astype(
-            jnp.float32
-        )
         damp_value = damping[which].astype(jnp.float32) * damping_factor
-        gain_start = gain_table[which]
         residual_before = residual[:, 0, :]
 
         def run(rounds):
             def branch(operands):
                 if rounds == 0:
-                    return (gain_start, residual_before)
+                    return (gain_table[which], residual_before)
                 return damped_rounds(
-                    rounds, gain_start, gain_start, residual_before, coher_now, onehot_p,
-                    onehot_q, damp_value, groups, nz,
+                    rounds, which, damp_value, gain_table, residual_before, coher_rows,
+                    onehot_p, onehot_q, groups, nz,
                 )
 
             return branch

time: 245 us -> 220 us (0.90)
  Pallas kernels: 191 us -> 172 us
  other arithmetic: 11.6 us -> 7.61 us
    pallas_call x4, Pallas kernels: 161 us -> 142 us  [damped_rounds(): pl.pallas_call(functools.partial(round_kernel, nb, nz, rounds), out_shape...]
where the time goes in v9:
time: 220 us; the launch traced here: 219 us
  Pallas kernels  172 us (78%)
  local copies, waits for them, and re-layouts  25.1 us (11%)
  loops' own time  13.5 us (6%)
  other arithmetic  7.61 us (3%)
    pallas_call x4, Pallas kernels, damped_rounds(): pl.pallas_call(functools.partial(round_kernel, nb, nz, rounds), out_shape...  142 us
    pallas_call x1, Pallas kernels, exchange_inputs(): pl.pallas_call(functools.partial(prologue_kernel, nb, nz), out_shape=(jax...  30.2 us
    another operation x1, loops' own time, on_device(): lax.fori_loop(0, SOLVED, sweep, (start, first_residual))  10.7 us

profile of v9, /device:TPU:1, one launch (start us, length us, event | category | flops | bytes accessed | tf_op | source)
XLA Modules:
  0.0 219.5 jit_solution(10829600428789788646)
XLA Ops:
  0.6 1.6 copy.77
  2.2 1.5 copy.61.gain_ref
  3.7 30.2 %shard_map.86 = (bf16[16,16,256]{2,1,0:T(8,128)(2,1)S(1)}, f32[32,32,128]{2,1,0:T(8,128)}) custom-call(bf16[16,16,256]{2,1,0:T(8,128)(2,1)} %bitcast.250, f32[32,128]{1,0:T(8,128)} %copy.61.gain_ref), custom_call_target="tpu_custom_call" | custom-call | tf_op jit(solution)/shard_map/pallas_call | solution.py:372
  33.9 1.6 copy.62
  36.2 1.2 copy_add_fusion
  37.5 0.9 copy.69
  38.4 2.0 gather_fusion.1
  40.4 1.5 copy.67
  42.1 2.0 gather_fusion
  44.1 1.5 copy.65
  46.3 171.2 %while.19 = (s32[]{:T(128)}, f32[32,8,512]{2,1,0:T(8,128)S(1)}, f32[8,1,256]{2,0,1:T(8,128)S(1)}, s32[32]{0:T(128)S(1)}, s32[32]{0:T(128)S(1)}, /*index=5*/s32[3...) while((s32[]{:T(128)}, f32[32,8,512]{2,1,0:T(8,128)S(1)}, ...), condition=%wide.region_6.8_spmd.clone, body=%wide.region_1.7_spmd.clone.sunk | while | flops 528412 | bytes 608735 | solution.py:452
  50.5 48.5 %conditional.3 = (f32[8,256]{1,0:T(8,128)S(1)}, f32[1,8,512]{2,1,0:T(8,128)S(1)}) conditional(s32[]{:T(128)} %bitcast.234, (s32[]{:T(128)}, f32[32,8,512]{2,1,0:T(8,128)S(1)}, f32[8,256]{1,0:T(8,128)S(1)}) %tuple.109, (s32[32]{0:T(128)S(1)}, s32[]{:T(128)}, s32[1]{0:T(128)}, f32[32,8,512]{2,1,0:T(8,128)S(1)}, ...), branch_computations={%region_3.4_spmd, %region_4.5_spmd, %region_5.6_spmd} | conditional | flops 3 | bytes 32822 | solution.py:447
  52.3 46.6 %branch_2_fun.2 = (f32[8,512]{1,0:T(8,128)S(1)}, f32[8,256]{1,0:T(8,128)S(1)}) custom-call(s32[1]{0:T(128)} %get-tuple-element.280.which_ref, f32[1,1]{1,0:T(1,128)} %bitcast.2.damp_ref, f32[32,8,512]{2,1,0:T(8,128)S(1)} %get-tuple-element.283.table_ref, f32[8,256]{1,0:T(8,128)} %copy.102.residual_ref, bf16[32,8,256]{2,1,0:T(8,128)(2,1)S(1)} %get-tuple-element.285.coher_ref, ...), custom_call_target="tpu_custom_call" | custom-call | tf_op jit(solution)/shard_map/while/body/eval_jaxpr/cond/branch_2_fun/pallas_call | solution.py:279
  99.0 0.7 and_reduce_fusion.2
  99.7 0.7 select_dynamic-update-slice_fusion.2
  104.3 28.0 %conditional.3 = (f32[8,256]{1,0:T(8,128)S(1)}, f32[1,8,512]{2,1,0:T(8,128)S(1)}) conditional(s32[]{:T(128)} %bitcast.234, (s32[]{:T(128)}, f32[32,8,512]{2,1,0:T(8,128)S(1)}, f32[8,256]{1,0:T(8,128)S(1)}) %tuple.109, (s32[32]{0:T(128)S(1)}, s32[]{:T(128)}, s32[1]{0:T(128)}, f32[32,8,512]{2,1,0:T(8,128)S(1)}, ...), branch_computations={%region_3.4_spmd, %region_4.5_spmd, %region_5.6_spmd} | conditional | flops 3 | bytes 32822 | solution.py:447
  106.2 26.1 %branch_1_fun.2 = (f32[8,512]{1,0:T(8,128)S(1)}, f32[8,256]{1,0:T(8,128)S(1)}) custom-call(s32[1]{0:T(128)} %get-tuple-element.270.which_ref, f32[1,1]{1,0:T(1,128)} %bitcast.damp_ref, f32[32,8,512]{2,1,0:T(8,128)S(1)} %get-tuple-element.273.table_ref, f32[8,256]{1,0:T(8,128)} %copy.101.residual_ref, bf16[32,8,256]{2,1,0:T(8,128)(2,1)S(1)} %get-tuple-element.275.coher_ref, ...), custom_call_target="tpu_custom_call" | custom-call | tf_op jit(solution)/shard_map/while/body/eval_jaxpr/cond/branch_1_fun/pallas_call | solution.py:279
  132.4 0.7 and_reduce_fusion.2
  137.7 28.0 %conditional.3 = (f32[8,256]{1,0:T(8,128)S(1)}, f32[1,8,512]{2,1,0:T(8,128)S(1)}) conditional(s32[]{:T(128)} %bitcast.234, (s32[]{:T(128)}, f32[32,8,512]{2,1,0:T(8,128)S(1)}, f32[8,256]{1,0:T(8,128)S(1)}) %tuple.109, (s32[32]{0:T(128)S(1)}, s32[]{:T(128)}, s32[1]{0:T(128)}, f32[32,8,512]{2,1,0:T(8,128)S(1)}, ...), branch_computations={%region_3.4_spmd, %region_4.5_spmd, %region_5.6_spmd} | conditional | flops 3 | bytes 32822 | solution.py:447
  139.5 26.2 %branch_1_fun.2 = (f32[8,512]{1,0:T(8,128)S(1)}, f32[8,256]{1,0:T(8,128)S(1)}) custom-call(s32[1]{0:T(128)} %get-tuple-element.270.which_ref, f32[1,1]{1,0:T(1,128)} %bitcast.damp_ref, f32[32,8,512]{2,1,0:T(8,128)S(1)} %get-tuple-element.273.table_ref, f32[8,256]{1,0:T(8,128)} %copy.101.residual_ref, bf16[32,8,256]{2,1,0:T(8,128)(2,1)S(1)} %get-tuple-element.275.coher_ref, ...), custom_call_target="tpu_custom_call" | custom-call | tf_op jit(solution)/shard_map/while/body/eval_jaxpr/cond/branch_1_fun/pallas_call | solution.py:279
  165.7 0.7 and_reduce_fusion.2
  171.0 45.1 %conditional.3 = (f32[8,256]{1,0:T(8,128)S(1)}, f32[1,8,512]{2,1,0:T(8,128)S(1)}) conditional(s32[]{:T(128)} %bitcast.234, (s32[]{:T(128)}, f32[32,8,512]{2,1,0:T(8,128)S(1)}, f32[8,256]{1,0:T(8,128)S(1)}) %tuple.109, (s32[32]{0:T(128)S(1)}, s32[]{:T(128)}, s32[1]{0:T(128)}, f32[32,8,512]{2,1,0:T(8,128)S(1)}, ...), branch_computations={%region_3.4_spmd, %region_4.5_spmd, %region_5.6_spmd} | conditional | flops 3 | bytes 32822 | solution.py:447
  172.9 43.2 %branch_2_fun.2 = (f32[8,512]{1,0:T(8,128)S(1)}, f32[8,256]{1,0:T(8,128)S(1)}) custom-call(s32[1]{0:T(128)} %get-tuple-element.280.which_ref, f32[1,1]{1,0:T(1,128)} %bitcast.2.damp_ref, f32[32,8,512]{2,1,0:T(8,128)S(1)} %get-tuple-element.283.table_ref, f32[8,256]{1,0:T(8,128)} %copy.102.residual_ref, bf16[32,8,256]{2,1,0:T(8,128)(2,1)S(1)} %get-tuple-element.285.coher_ref, ...), custom_call_target="tpu_custom_call" | custom-call | tf_op jit(solution)/shard_map/while/body/eval_jaxpr/cond/branch_2_fun/pallas_call | solution.py:279
  216.2 0.7 and_reduce_fusion.2
  (60 shorter events, 15.2 us)
Async XLA Ops:
  35.6 0.7 copy-start.3
  37.4 0.9 copy-start.2
  45.6 0.7 copy-start.1
  45.6 0.7 copy-start
  45.6 0.7 copy-start.4
  45.6 0.7 copy-start.5
  45.6 0.7 copy-start.6

commit v10 on v9

--- a/solution.py
+++ b/solution.py
@@ -115,7 +115,7 @@
 
 def round_kernel(
     nb, nz, rounds, which_ref, damp_ref, table_ref, residual_ref, coher_ref, onehot_p_ref,
-    onehot_q_ref, o_ref, res_out, pay, r1, r2, r3, s1, q1, s2, q2, s3, q3,
+    onehot_q_ref, table_out, res_out, pay, r1, r2, r3, s1, q1, s2, q2, s3, q3,
 ):
     mz = lax.axis_index("dir")
     mb = lax.axis_index("bl")
@@ -239,7 +239,8 @@
         local_sums(gain_now)
         all_reduce(r)
         gain_now = solve(gain_now, groups, pairs, r)
-    o_ref[...] = gain_now
+    for d in range(table_ref.shape[0]):
+        table_out[d] = jnp.where(which == d, gain_now, table_ref[d])
     final_model = model_rows(split_three(gain_now), coher_now, onehot_p, onehot_q)
     res_out[...] = jnp.concatenate([target[i] - final_model[i] for i in range(8)], 0)
 
@@ -279,7 +280,7 @@
     return pl.pallas_call(
         functools.partial(round_kernel, nb, nz, rounds),
         out_shape=(
-            jax.ShapeDtypeStruct(gain_table.shape[1:], gain_table.dtype),
+            jax.ShapeDtypeStruct(gain_table.shape, gain_table.dtype),
             jax.ShapeDtypeStruct(residual.shape, residual.dtype),
         ),
         in_specs=[smem, smem] + [vmem] * 5,
@@ -430,26 +431,25 @@
         gain_table, residual = state
         which = solve_order[step_index]
         damp_value = damping[which].astype(jnp.float32) * damping_factor
-        residual_before = residual[:, 0, :]
 
         def run(rounds):
             def branch(operands):
                 if rounds == 0:
-                    return (gain_table[which], residual_before)
+                    return (gain_table, residual)
                 return damped_rounds(
-                    rounds, which, damp_value, gain_table, residual_before, coher_rows,
+                    rounds, which, damp_value, gain_table, residual, coher_rows,
                     onehot_p, onehot_q, groups, nz,
                 )
 
             return branch
 
         rounds = jnp.clip(counts[which], 0, LM_ITERS)
-        gain_final, residual_after = lax.switch(
-            rounds, [run(r) for r in range(LM_ITERS + 1)], None
-        )
-        return (gain_table.at[which].set(gain_final), residual_after[:, None, :])
-
-    gain_table, residual = lax.fori_loop(0, SOLVED, sweep, (start, first_residual))
+        return lax.switch(rounds, [run(r) for r in range(LM_ITERS + 1)], None)
+
+    gain_table, residual_rows = lax.fori_loop(
+        0, SOLVED, sweep, (start, first_residual[:, 0, :])
+    )
+    residual = residual_rows[:, None, :]
     own_width = station_count // groups
     gains = lax.dynamic_slice_in_dim(gain_table, lax.axis_index("bl") * own_width, own_width, 2)
     return (gains, residual)

time: 220 us -> 203 us (0.923)
  Pallas kernels: 172 us -> 157 us
  other arithmetic: 7.61 us -> 2.16 us
  local copies, waits for them, and re-layouts: 25.1 us -> 28.2 us
    pallas_call x4, Pallas kernels: 142 us -> 127 us  [damped_rounds(): pl.pallas_call(functools.partial(round_kernel, nb, nz, rounds), out_shape...]
    cond x4 -> x8, local copies, waits for them, and re-layouts: 2.41 us -> 5.59 us
    another operation x4 -> x0, other arithmetic: 2.84 us -> none
    scatter x4 -> x0, other arithmetic: 2.61 us -> none  [sweep(): return (gain_table.at[which].set(gain_final), residual_after[:, None, :])]
where the time goes in v10:
time: 203 us; the launch traced here: 202 us
  Pallas kernels  157 us (77%)
  local copies, waits for them, and re-layouts  28.2 us (14%)
  loops' own time  13.5 us (7%)
  other arithmetic  2.16 us (1%)
    pallas_call x4, Pallas kernels, damped_rounds(): pl.pallas_call(functools.partial(round_kernel, nb, nz, rounds), out_shape...  127 us
    pallas_call x1, Pallas kernels, exchange_inputs(): pl.pallas_call(functools.partial(prologue_kernel, nb, nz), out_shape=(jax...  30.2 us
    another operation x1, loops' own time, on_device(): lax.fori_loop(0, SOLVED, sweep, (start, first_residual[:, 0, :]))  10.7 us
    cond x8, local copies, waits for them, and re-layouts  5.59 us

profile of v10, /device:TPU:1, one launch (start us, length us, event | category | flops | bytes accessed | tf_op | source)
XLA Modules:
  0.0 201.9 jit_solution(8011123364800139432)
XLA Ops:
  0.6 1.6 copy.73
  2.2 1.5 copy.58.gain_ref
  3.7 30.2 %shard_map.86 = (bf16[16,16,256]{2,1,0:T(8,128)(2,1)S(1)}, f32[32,32,128]{2,1,0:T(8,128)}) custom-call(bf16[16,16,256]{2,1,0:T(8,128)(2,1)} %bitcast.237, f32[32,128]{1,0:T(8,128)} %copy.58.gain_ref), custom_call_target="tpu_custom_call" | custom-call | tf_op jit(solution)/shard_map/pallas_call | solution.py:373
  33.9 1.6 copy.59
  36.2 1.2 copy_add_fusion
  37.5 0.9 copy.66
  38.4 2.0 gather_fusion.1
  40.4 1.5 copy.64
  42.0 2.0 gather_fusion
  44.0 1.5 copy.62
  46.3 153.7 %while.18 = (s32[]{:T(128)}, f32[32,8,512]{2,1,0:T(8,128)S(1)}, f32[8,256]{1,0:T(8,128)S(1)}, s32[32]{0:T(128)S(1)}, s32[32]{0:T(128)S(1)}, /*index=5*/s32[32]{0...) while((s32[]{:T(128)}, f32[32,8,512]{2,1,0:T(8,128)S(1)}, ...), condition=%wide.region_5.7_spmd.clone, body=%wide.region_1.6_spmd.clone.sunk | while | flops 524298 | bytes 1591655 | solution.py:449
  50.4 29.1 %conditional.3 = ((f32[32,8,512]{2,1,0:T(8,128)S(1)}, f32[8,256]{1,0:T(8,128)S(1)})) conditional(s32[]{:T(128)} %bitcast.230, (f32[32,8,512]{2,1,0:T(8,128)S(1)}, f32[8,256]{1,0:T(8,128)S(1)}) %tuple.80, (s32[32]{0:T(128)S(1)}, s32[]{:T(128)}, s32[1]{0:T(128)}, f32[32,8,512]{2,1,0:T(8,128)S(1)}, f32[8,256]{1,0:T(8,128)S(1)}, ...), branch_computations={%region_2.3_spmd, %region_3.4_spmd, %region_4.5_spmd} | conditional | flops 2 | bytes 1065000 | solution.py:447
  51.7 0.8 copy.96.table_ref
  53.1 26.4 %branch_1_fun.2 = (f32[32,8,512]{2,1,0:T(8,128)S(1)}, f32[8,256]{1,0:T(8,128)S(1)}) custom-call(s32[1]{0:T(128)} %get-tuple-element.238.which_ref, f32[1,1]{1,0:T(1,128)} %bitcast.damp_ref, f32[32,8,512]{2,1,0:T(8,128)} %copy.96.table_ref, f32[8,256]{1,0:T(8,128)} %copy.97.residual_ref, bf16[32,8,256]{2,1,0:T(8,128)(2,1)S(1)} %get-tuple-element.243.coher_ref, ...), custom_call_target="tpu_custom_call" | custom-call | tf_op jit(solution)/shard_map/while/body/eval_jaxpr/cond/branch_1_fun/pallas_call | solution.py:280
  83.5 29.1 %conditional.3 = ((f32[32,8,512]{2,1,0:T(8,128)S(1)}, f32[8,256]{1,0:T(8,128)S(1)})) conditional(s32[]{:T(128)} %bitcast.230, (f32[32,8,512]{2,1,0:T(8,128)S(1)}, f32[8,256]{1,0:T(8,128)S(1)}) %tuple.80, (s32[32]{0:T(128)S(1)}, s32[]{:T(128)}, s32[1]{0:T(128)}, f32[32,8,512]{2,1,0:T(8,128)S(1)}, f32[8,256]{1,0:T(8,128)S(1)}, ...), branch_computations={%region_2.3_spmd, %region_3.4_spmd, %region_4.5_spmd} | conditional | flops 2 | bytes 1065000 | solution.py:447
  84.8 0.8 copy.96.table_ref
  86.2 26.4 %branch_1_fun.2 = (f32[32,8,512]{2,1,0:T(8,128)S(1)}, f32[8,256]{1,0:T(8,128)S(1)}) custom-call(s32[1]{0:T(128)} %get-tuple-element.238.which_ref, f32[1,1]{1,0:T(1,128)} %bitcast.damp_ref, f32[32,8,512]{2,1,0:T(8,128)} %copy.96.table_ref, f32[8,256]{1,0:T(8,128)} %copy.97.residual_ref, bf16[32,8,256]{2,1,0:T(8,128)(2,1)S(1)} %get-tuple-element.243.coher_ref, ...), custom_call_target="tpu_custom_call" | custom-call | tf_op jit(solution)/shard_map/while/body/eval_jaxpr/cond/branch_1_fun/pallas_call | solution.py:280
  116.6 29.3 %conditional.3 = ((f32[32,8,512]{2,1,0:T(8,128)S(1)}, f32[8,256]{1,0:T(8,128)S(1)})) conditional(s32[]{:T(128)} %bitcast.230, (f32[32,8,512]{2,1,0:T(8,128)S(1)}, f32[8,256]{1,0:T(8,128)S(1)}) %tuple.80, (s32[32]{0:T(128)S(1)}, s32[]{:T(128)}, s32[1]{0:T(128)}, f32[32,8,512]{2,1,0:T(8,128)S(1)}, f32[8,256]{1,0:T(8,128)S(1)}, ...), branch_computations={%region_2.3_spmd, %region_3.4_spmd, %region_4.5_spmd} | conditional | flops 2 | bytes 1065000 | solution.py:447
  117.8 0.8 copy.96.table_ref
  119.2 26.6 %branch_1_fun.2 = (f32[32,8,512]{2,1,0:T(8,128)S(1)}, f32[8,256]{1,0:T(8,128)S(1)}) custom-call(s32[1]{0:T(128)} %get-tuple-element.238.which_ref, f32[1,1]{1,0:T(1,128)} %bitcast.damp_ref, f32[32,8,512]{2,1,0:T(8,128)} %copy.96.table_ref, f32[8,256]{1,0:T(8,128)} %copy.97.residual_ref, bf16[32,8,256]{2,1,0:T(8,128)(2,1)S(1)} %get-tuple-element.243.coher_ref, ...), custom_call_target="tpu_custom_call" | custom-call | tf_op jit(solution)/shard_map/while/body/eval_jaxpr/cond/branch_1_fun/pallas_call | solution.py:280
  149.8 50.2 %conditional.3 = ((f32[32,8,512]{2,1,0:T(8,128)S(1)}, f32[8,256]{1,0:T(8,128)S(1)})) conditional(s32[]{:T(128)} %bitcast.230, (f32[32,8,512]{2,1,0:T(8,128)S(1)}, f32[8,256]{1,0:T(8,128)S(1)}) %tuple.80, (s32[32]{0:T(128)S(1)}, s32[]{:T(128)}, s32[1]{0:T(128)}, f32[32,8,512]{2,1,0:T(8,128)S(1)}, f32[8,256]{1,0:T(8,128)S(1)}, ...), branch_computations={%region_2.3_spmd, %region_3.4_spmd, %region_4.5_spmd} | conditional | flops 2 | bytes 1065000 | solution.py:447
  151.1 0.8 copy.98.table_ref
  152.5 47.5 %branch_2_fun.2 = (f32[32,8,512]{2,1,0:T(8,128)S(1)}, f32[8,256]{1,0:T(8,128)S(1)}) custom-call(s32[1]{0:T(128)} %get-tuple-element.246.which_ref, f32[1,1]{1,0:T(1,128)} %bitcast.1.damp_ref, f32[32,8,512]{2,1,0:T(8,128)} %copy.98.table_ref, f32[8,256]{1,0:T(8,128)} %copy.99.residual_ref, bf16[32,8,256]{2,1,0:T(8,128)(2,1)S(1)} %get-tuple-element.251.coher_ref, ...), custom_call_target="tpu_custom_call" | custom-call | tf_op jit(solution)/shard_map/while/body/eval_jaxpr/cond/branch_2_fun/pallas_call | solution.py:280
  200.0 0.6 copy.67
  (54 shorter events, 12.6 us)
Async XLA Ops:
  35.6 0.7 copy-start.2
  37.4 0.9 copy-start.1
  45.6 0.7 copy-start
  45.6 0.7 copy-start.3
  45.6 0.7 copy-start.4
  45.6 0.7 copy-start.5
